TPU v7x, 256 devices: a whole 4x4x8 slice. The times are simulated.
256 devices in a mesh: ta: 64 (over x, y, z_lo, core), gz: 4 (over z_hi).
Axes of the slice: x: 4, y: 4, z: 8 (z_hi: 4, z_lo: 2; z = z_hi * 2 + z_lo), core: 2. Of those that a mesh axis runs over, the one named last changes fastest.
Arguments:
- links: float32 [4, 18, 4, 512, 256], P(None, None, 'gz', 'ta'), may hold values from -1 to 1, as said below
- source: float32 [24, 4, 512, 256], P(None, 'gz', 'ta'), may hold values from -6 to 6
Outputs:
- solution: float32 [24, 4, 512, 256], P(None, 'gz', 'ta')
- residual: float32 [24, 4, 512, 256], P(None, 'gz', 'ta')
Inputs may be any that keep to these rules, and one draw needn't show every extreme that they name: `links`: every link is a unitary 3x3 complex matrix.
All inputs are finite; a program needn't handle non-finite values.
Results may differ from a plain program's by a relative error of at most 0.00027.
Values sent between devices are 32-bit elements; how exact they have to be, the bound alone decides.
No kernel may reach another device: no remote copies, remote signals or barrier semaphores. Data moves between devices by JAX's collectives and lax.ppermute only.
A program may use at most 256 MiB of HBM per device.

v0:
```python
import jax
import jax.numpy as jnp
from jax import lax
from jax.experimental import pallas as pl
from jax.experimental.pallas import tpu as pltpu
from jax.sharding import PartitionSpec as P


NMR = 4
DIAGONAL = 4.0 + 0.2
EPSILON = 1e-06
ENTRIES = 12 * 8 * 8 * 8
X, Y, Z, T = 0, 1, 2, 3
COLUMN = ((3, 2, 1, 0), (3, 2, 1, 0), (2, 3, 0, 1), (2, 3, 0, 1))
REAL = ((0, 0, 0, 0), (-1, 1, 1, -1), (0, 0, 0, 0), (1, 1, 1, 1))
IMAG = ((1, 1, -1, -1), (0, 0, 0, 0), (1, -1, -1, 1), (0, 0, 0, 0))
TILE = (8, 128)
F32 = jnp.float32


def lane_ids():
    return lax.broadcasted_iota(jnp.int32, TILE, 1)


def time_ids():
    return lax.broadcasted_iota(jnp.int32, TILE, 0)


def my_parity():
    return (lax.axis_index("gz") + lax.axis_index("ta")) % 2


def row_zero_first():
    return (lane_ids() // 8) % 2 == my_parity()


def is_even(axis):
    return (lane_ids() * 0 + lax.axis_index(axis)) % 2 == 0


def lanes_by(value, steps):
    return pltpu.roll(value, steps % 128, 1)


def times_by(value, steps):
    return pltpu.roll(value, steps % 8, 0)


def add_gamma(base, orientation, direction, row, value):
    real = orientation * REAL[direction][row]
    imag = orientation * IMAG[direction][row]
    if real > 0:
        return (base[0] + value[0], base[1] + value[1])
    if real < 0:
        return (base[0] - value[0], base[1] - value[1])
    if imag > 0:
        return (base[0] - value[1], base[1] + value[0])
    return (base[0] + value[1], base[1] - value[0])


def project(field, direction, orientation):
    return [
        [
            add_gamma(
                field[row][color], orientation, direction, row, field[COLUMN[direction][row]][color]
            )
            for color in range(3)
        ]
        for row in range(2)
    ]


def expand_into(total, half, direction, orientation):
    for row in range(4):
        for color in range(3):
            if row < 2:
                base, value = total[row][color], half[row][color]
                total[row][color] = (base[0] + value[0], base[1] + value[1])
            else:
                total[row][color] = add_gamma(
                    total[row][color],
                    orientation,
                    direction,
                    row,
                    half[COLUMN[direction][row]][color],
                )


def color_apply(link, half, adjoint):
    result = []
    for row in range(2):
        out = []
        for a in range(3):
            real, imag = None, None
            for b in range(3):
                value = half[row][b]
                entry = link[b][a] if adjoint else link[a][b]
                if adjoint:
                    pr = entry[0] * value[0] + entry[1] * value[1]
                    pi = entry[0] * value[1] - entry[1] * value[0]
                else:
                    pr = entry[0] * value[0] - entry[1] * value[1]
                    pi = entry[0] * value[1] + entry[1] * value[0]
                real = pr if real is None else real + pr
                imag = pi if imag is None else imag + pi
            out.append((real, imag))
        result.append(out)
    return result


def map_half(function, half):
    return [[(function(v[0]), function(v[1])) for v in row] for row in half]


def load_link(get):
    return [[(get(a * 3 + b), get(9 + a * 3 + b)) for b in range(3)] for a in range(3)]


def load_spinor(ref):
    return [[(ref[s * 3 + c], ref[12 + s * 3 + c]) for c in range(3)] for s in range(4)]


def store_spinor(ref, field):
    for s in range(4):
        for c in range(3):
            ref[s * 3 + c] = field[s][c][0]
            ref[12 + s * 3 + c] = field[s][c][1]


def flat_half(half):
    return [half[s][c][part] for part in range(2) for s in range(2) for c in range(3)]


def unflat_half(flat):
    return [[(flat[s * 3 + c], flat[6 + s * 3 + c]) for c in range(3)] for s in range(2)]


def scaled(field, factor):
    return [[(factor * v[0], factor * v[1]) for v in row] for row in field]


def compact(ref, index, color, first):
    low = ref[index, :, 0:128]
    high = ref[index, :, 128:256]
    return jnp.where(first, low, high) if color == 0 else jnp.where(first, high, low)


def solve(rho_ref, w_ref, applied_ref, masked_ref, link):
    lane, time = lane_ids(), time_ids()
    inner = {X: lane % 8 != 7, Y: lane < 112, T: time != 7}
    for slot, direction in enumerate((X, Y, T)):
        for i in range(18):
            masked_ref[slot * 18 + i] = jnp.where(
                inner[direction], -0.5 * link(direction, i), 0.0
            )
    ahead = {
        X: lambda v: lanes_by(v, -1),
        Y: lambda v: lanes_by(v, -16),
        T: lambda v: times_by(v, -1),
    }
    behind = {
        X: lambda v: lanes_by(v, 1),
        Y: lambda v: lanes_by(v, 16),
        T: lambda v: times_by(v, 1),
    }
    left = (lane // 8) % 2 == 0

    def per_block(value):
        total_left = jnp.sum(jnp.where(left, value, 0.0), axis=(0, 1), keepdims=True)
        total_right = jnp.sum(jnp.where(left, 0.0, value), axis=(0, 1), keepdims=True)
        return jnp.where(left, total_left, total_right) / ENTRIES

    def step(_, carry):
        rho = load_spinor(rho_ref)
        total = scaled(rho, DIAGONAL)
        for slot, direction in enumerate((X, Y, T)):
            matrix = load_link(lambda i: masked_ref[slot * 18 + i])
            half = map_half(ahead[direction], project(rho, direction, -1))
            expand_into(total, color_apply(matrix, half, False), direction, -1)
            half = color_apply(matrix, project(rho, direction, 1), True)
            expand_into(total, map_half(behind[direction], half), direction, 1)
        store_spinor(applied_ref, total)
        real, imag, square = None, None, None
        for s in range(4):
            for c in range(3):
                (ar, ai), (rr, ri) = total[s][c], rho[s][c]
                pr = ar * rr + ai * ri
                pi = ar * ri - ai * rr
                ps = ar * ar + ai * ai
                real = pr if real is None else real + pr
                imag = pi if imag is None else imag + pi
                square = ps if square is None else square + ps
        denominator = per_block(square) + EPSILON
        weight_real = per_block(real) / denominator
        weight_imag = per_block(imag) / denominator
        for i in range(12):
            rr, ri = rho_ref[i], rho_ref[12 + i]
            ar, ai = applied_ref[i], applied_ref[12 + i]
            w_ref[i] = w_ref[i] + (weight_real * rr - weight_imag * ri)
            w_ref[12 + i] = w_ref[12 + i] + (weight_real * ri + weight_imag * rr)
            rho_ref[i] = rr - (weight_real * ar - weight_imag * ai)
            rho_ref[12 + i] = ri - (weight_real * ai + weight_imag * ar)
        return carry

    for i in range(24):
        w_ref[i] = jnp.zeros(TILE, F32)
    lax.fori_loop(0, NMR, step, 0)


def add_local_hops(total, half_w, link_to, link_from):
    lane = lane_ids()
    column = lane % 16

    def x_ahead(v):
        near = jnp.where(column == 7, lanes_by(v, -1), 0.0)
        return jnp.where(column == 15, lanes_by(v, 15), near)

    def x_behind(v):
        near = jnp.where(column == 8, lanes_by(v, 1), 0.0)
        return jnp.where(column == 0, lanes_by(v, -15), near)

    def y_ahead(v):
        return jnp.where(lane >= 112, lanes_by(v, -16), 0.0)

    def y_behind(v):
        return jnp.where(lane < 16, lanes_by(v, 16), 0.0)

    for direction, ahead, behind in ((X, x_ahead, x_behind), (Y, y_ahead, y_behind)):
        half = map_half(ahead, project(half_w, direction, -1))
        matrix = load_link(lambda i: link_to(direction, i))
        expand_into(total, color_apply(matrix, half, False), direction, -1)
        matrix = load_link(lambda i: link_from(direction, i))
        half = map_half(behind, color_apply(matrix, project(half_w, direction, 1), True))
        expand_into(total, half, direction, 1)


def outgoing(half_w, link_from, direction):
    matrix = load_link(lambda i: link_from(direction, i))
    ahead = color_apply(matrix, project(half_w, direction, 1), True)
    behind = project(half_w, direction, -1)
    return flat_half(ahead), flat_half(behind)


def store_pairs(even, ahead, behind, first_ref, second_ref):
    for i in range(len(ahead)):
        first_ref[i] = jnp.where(even, ahead[i], behind[i])
        second_ref[i] = jnp.where(even, behind[i], ahead[i])


def load_pairs(even, first, second):
    low = [jnp.where(even, b, a) for a, b in zip(first, second)]
    high = [jnp.where(even, a, b) for a, b in zip(first, second)]
    return low, high


def store_rows(ref, index, row):
    ref[index : index + 1, :] = row


def row_at(ref, time):
    here = time_ids() == time
    return unflat_half(
        [jnp.where(here, jnp.broadcast_to(ref[i : i + 1, :], TILE), 0.0) for i in range(12)]
    )


def store_faces(half_w, depth_half_w, link_from, t_refs, z_refs):
    ahead, behind = outgoing(depth_half_w, link_from, Z)
    store_pairs(is_even("gz"), ahead, behind, *z_refs)
    ahead, behind = outgoing(half_w, link_from, T)
    even = is_even("ta")[0:1, :]
    for i in range(12):
        low, high = behind[i][0:1, :], ahead[i][7:8, :]
        store_rows(t_refs[0], i, jnp.where(even, high, low))
        store_rows(t_refs[1], i, jnp.where(even, low, high))


def add_faces(total, link_to, t_refs, z_refs):
    low, high = load_pairs(
        is_even("gz"), [z_refs[0][i] for i in range(12)], [z_refs[1][i] for i in range(12)]
    )
    expand_into(total, unflat_half(low), Z, 1)
    matrix = load_link(lambda i: link_to(Z, i))
    expand_into(total, color_apply(matrix, unflat_half(high), False), Z, -1)
    time = time_ids()
    rows = [
        [jnp.broadcast_to(ref[i : i + 1, :], TILE) for i in range(12)] for ref in t_refs
    ]
    low, high = load_pairs(is_even("ta"), *rows)
    low = unflat_half([jnp.where(time == 0, v, 0.0) for v in low])
    high = unflat_half([jnp.where(time == 7, v, 0.0) for v in high])
    expand_into(total, low, T, 1)
    matrix = load_link(lambda i: link_to(T, i))
    expand_into(total, color_apply(matrix, high, False), T, -1)


def packed_lower(flat):
    low = time_ids() < 4
    return [jnp.where(low, flat[i + 6], times_by(flat[i], 4)) for i in range(6)]


def unpacked_lower(tiles):
    low = time_ids() < 4
    flat = [jnp.where(low, 0.0, v) for v in tiles]
    flat += [jnp.where(low, 0.0, times_by(v, 4)) for v in tiles]
    return unflat_half(flat)


def packed_split(flat):
    low = time_ids() < 4
    stay, move = [], []
    for i in range(6):
        turned = times_by(flat[i], 4)
        stay.append(jnp.where(low, turned, flat[i + 6]))
        move.append(jnp.where(low, flat[i + 6], turned))
    return stay, move


def join_split(low_tiles, high_tiles):
    low = time_ids() < 4
    flat = [jnp.where(low, a, b) for a, b in zip(low_tiles, high_tiles)]
    flat += [times_by(jnp.where(low, b, a), 4) for a, b in zip(low_tiles, high_tiles)]
    return unflat_half(flat)


def zero_spinor():
    zero = jnp.zeros(TILE, F32)
    return [[(zero, zero) for _ in range(3)] for _ in range(4)]


def masked_spinor(field, mask):
    return [[(jnp.where(mask, v[0], 0.0), jnp.where(mask, v[1], 0.0)) for v in row] for row in field]


def add_spinor(total, other):
    for s in range(4):
        for c in range(3):
            a, b = total[s][c], other[s][c]
            total[s][c] = (a[0] + b[0], a[1] + b[1])


def raw_links(links_ref):
    first = row_zero_first()
    return [
        lambda direction, i, color=color: compact(links_ref, direction * 18 + i, color, first)
        for color in range(2)
    ]


def fill_moved_links(moved_ref, links_ref, received_ref):
    first = row_zero_first()
    low = time_ids() < 4
    for i in range(72):
        zero = times_by(compact(links_ref, i, 0, first), 4)
        one = times_by(compact(links_ref, i, 1, first), 4)
        other = received_ref[i]
        moved_ref[i] = jnp.where(low, other, zero)
        moved_ref[72 + i] = jnp.where(low, times_by(other, 4), one)


def moved_links(moved_ref):
    return [
        lambda direction, i, color=color: moved_ref[72 * color + direction * 18 + i]
        for color in range(2)
    ]


def pack_links_kernel(links_ref, out_ref):
    first = row_zero_first()
    low = time_ids() < 4
    for i in range(72):
        zero = compact(links_ref, i, 0, first)
        one = compact(links_ref, i, 1, first)
        out_ref[i] = jnp.where(low, times_by(one, 4), zero)


def kernel_one(links_ref, source_ref, w_ref, rho_ref, other_ref, t0_ref, t1_ref, z0_ref, z1_ref,
               applied_ref, masked_ref):
    first = row_zero_first()
    link = raw_links(links_ref)
    for i in range(24):
        rho_ref[i] = compact(source_ref, i, 0, first)
        other_ref[i] = compact(source_ref, i, 1, first)
    solve(rho_ref, w_ref, applied_ref, masked_ref, link[0])
    half_w = scaled(load_spinor(w_ref), 0.5)
    store_faces(half_w, half_w, link[0], (t0_ref, t1_ref), (z0_ref, z1_ref))
    total = load_spinor(other_ref)
    add_local_hops(total, half_w, link[1], link[0])
    store_spinor(other_ref, total)


def kernel_two(links_ref, rho_in, other_in, t0_in, t1_in, z0_in, z1_in,
               w_ref, rest_ref, rho_ref, send_ref, tb_ref, z0_ref, z1_ref,
               applied_ref, masked_ref):
    link = raw_links(links_ref)
    total = load_spinor(other_in)
    add_faces(total, link[1], (t0_in, t1_in), (z0_in, z1_in))
    store_spinor(rho_ref, total)
    solve(rho_ref, w_ref, applied_ref, masked_ref, link[1])
    half_w = scaled(load_spinor(w_ref), 0.5)
    ahead, behind = outgoing(half_w, link[1], Z)
    store_pairs(is_even("gz"), packed_lower(ahead), packed_lower(behind), z0_ref, z1_ref)
    behind = flat_half(project(half_w, T, -1))
    for i in range(12):
        store_rows(tb_ref, i, behind[i][0:1, :])
    total = load_spinor(rho_in)
    add_local_hops(total, half_w, link[0], link[1])
    store_spinor(rest_ref, total)
    low = time_ids() < 4
    for i in range(24):
        send_ref[i] = jnp.where(low, times_by(rho_ref[i], 4), rest_ref[i])
    for i in range(12):
        send_ref[24 + i] = jnp.where(low, times_by(w_ref[i], 4), w_ref[12 + i])


def kernel_three(links_ref, moved_in, rest_in, rho_in, tb_in, received, z0_in, z1_in,
                 w_ref, rho_ref, other_ref, t0_ref, t1_ref, z0_ref, z1_ref,
                 applied_ref, masked_ref, moved_ref):
    fill_moved_links(moved_ref, links_ref, moved_in)
    link = moved_links(moved_ref)
    time = time_ids()
    low = time < 4
    for i in range(24):
        other = received[i]
        rho_ref[i] = jnp.where(low, other, times_by(rest_in[i], 4))
        other_ref[i] = jnp.where(low, times_by(other, 4), times_by(rho_in[i], 4))
    came = [jnp.where(low, 0.5 * received[24 + i], 0.0) for i in range(12)]
    came += [jnp.where(low, 0.5 * times_by(received[24 + i], 4), 0.0) for i in range(12)]
    came = [[(came[s * 3 + c], came[12 + s * 3 + c]) for c in range(3)] for s in range(4)]
    total = load_spinor(rho_ref)
    lower, higher = load_pairs(
        is_even("gz"), [z0_in[i] for i in range(6)], [z1_in[i] for i in range(6)]
    )
    expand_into(total, unpacked_lower(lower), Z, 1)
    matrix = load_link(lambda i: link[0](Z, i))
    expand_into(total, color_apply(matrix, unpacked_lower(higher), False), Z, -1)
    matrix = load_link(lambda i: link[0](T, i))
    half = color_apply(matrix, project(came, T, 1), True)
    half = map_half(lambda v: jnp.where(time == 4, times_by(v, 1), 0.0), half)
    expand_into(total, half, T, 1)
    store_spinor(rho_ref, total)
    total = load_spinor(other_ref)
    matrix = load_link(lambda i: link[1](T, i))
    expand_into(total, color_apply(matrix, row_at(tb_in, 3), False), T, -1)
    store_spinor(other_ref, total)
    solve(rho_ref, w_ref, applied_ref, masked_ref, link[0])
    half_w = scaled(load_spinor(w_ref), 0.5)
    depth_half_w = came
    add_spinor(depth_half_w, half_w)
    store_faces(half_w, depth_half_w, link[0], (t0_ref, t1_ref), (z0_ref, z1_ref))
    total = load_spinor(other_ref)
    add_local_hops(total, half_w, link[1], link[0])
    store_spinor(other_ref, total)


def kernel_four(links_ref, moved_in, w_in, rho_in, other_in, t0_in, t1_in, z0_in, z1_in,
                w_ref, rest_ref, rho_ref, send_ref, ta_ref, z0_ref, z1_ref, za_ref, zb_ref,
                applied_ref, masked_ref, moved_ref):
    fill_moved_links(moved_ref, links_ref, moved_in)
    link = moved_links(moved_ref)
    total = load_spinor(other_in)
    add_faces(total, link[1], (t0_in, t1_in), (z0_in, z1_in))
    store_spinor(rho_ref, total)
    solve(rho_ref, w_ref, applied_ref, masked_ref, link[1])
    half_w = scaled(load_spinor(w_ref), 0.5)
    ahead, behind = outgoing(half_w, link[1], Z)
    ahead, ahead_move = packed_split(ahead)
    behind, behind_move = packed_split(behind)
    store_pairs(is_even("gz"), ahead, behind, z0_ref, z1_ref)
    for i in range(6):
        za_ref[i] = ahead_move[i]
        zb_ref[i] = behind_move[i]
    matrix = load_link(lambda i: link[1](T, i))
    ahead = flat_half(color_apply(matrix, project(half_w, T, 1), True))
    for i in range(12):
        store_rows(ta_ref, i, ahead[i][7:8, :])
    total = load_spinor(rho_in)
    add_local_hops(total, half_w, link[0], link[1])
    store_spinor(rest_ref, total)
    low = time_ids() < 4
    for i in range(24):
        send_ref[i] = jnp.where(low, rho_ref[i], times_by(rest_ref[i], 4))
        send_ref[24 + i] = jnp.where(low, w_ref[i], times_by(w_in[i], 4))


def kernel_five(links_ref, w0_ref, w1_ref, x0_ref, x1_ref, rest_in, rho_in, ta_in, received,
                z0_in, z1_in, za_in, zb_in, solution_ref, residual_ref):
    link = raw_links(links_ref)
    first = row_zero_first()
    time = time_ids()
    low = time < 4

    def put(ref, i, zero, one):
        ref[i, :, 0:128] = jnp.where(first, zero, one)
        ref[i, :, 128:256] = jnp.where(first, one, zero)

    update = []
    for i in range(24):
        other = received[24 + i]
        zero = jnp.where(low, times_by(x0_ref[i], 4), times_by(other, 4))
        one = jnp.where(low, times_by(x1_ref[i], 4), other)
        put(solution_ref, i, w0_ref[i] + zero, w1_ref[i] + one)
        update.append(zero)
    lower, higher = load_pairs(
        is_even("gz"), [z0_in[i] for i in range(6)], [z1_in[i] for i in range(6)]
    )
    faces = zero_spinor()
    expand_into(faces, join_split(lower, [za_in[i] for i in range(6)]), Z, 1)
    matrix = load_link(lambda i: jnp.where(low, link[0](Z, i), link[1](Z, i)))
    half = join_split(higher, [zb_in[i] for i in range(6)])
    expand_into(faces, color_apply(matrix, half, False), Z, -1)
    zero, one = masked_spinor(faces, low), masked_spinor(faces, jnp.logical_not(low))
    update = [
        [(0.5 * update[s * 3 + c], 0.5 * update[12 + s * 3 + c]) for c in range(3)] for s in range(4)
    ]
    half = map_half(
        lambda v: jnp.where(time == 3, times_by(v, -1), 0.0), project(update, T, -1)
    )
    matrix = load_link(lambda i: link[0](T, i))
    expand_into(zero, color_apply(matrix, half, False), T, -1)
    expand_into(one, row_at(ta_in, 4), T, 1)
    for s in range(4):
        for c in range(3):
            for part in range(2):
                i = part * 12 + s * 3 + c
                other = received[i]
                base_zero = jnp.where(low, times_by(rest_in[i], 4), times_by(other, 4))
                base_one = jnp.where(low, times_by(rho_in[i], 4), other)
                put(residual_ref, i, base_zero + zero[s][c][part], base_one + one[s][c][part])


def call(kernel, shapes, operands, solver=False, moved=False, cost=3000000):
    scratch = []
    if solver:
        scratch = [pltpu.VMEM((24,) + TILE, F32), pltpu.VMEM((54,) + TILE, F32)]
    if moved:
        scratch.append(pltpu.VMEM((144,) + TILE, F32))
    vmem = pl.BlockSpec(memory_space=pltpu.VMEM)
    return pl.pallas_call(
        kernel,
        out_shape=[jax.ShapeDtypeStruct(shape, F32) for shape in shapes],
        in_specs=[vmem] * len(operands),
        out_specs=[vmem] * len(shapes),
        scratch_shapes=scratch,
        compiler_params=pltpu.CompilerParams(vmem_limit_bytes=12 << 20),
        cost_estimate=pl.CostEstimate(flops=cost, bytes_accessed=cost // 2, transcendentals=0),
    )(*operands)


def moved_to(value, time_steps, depth_steps):
    times, depths = lax.axis_size("ta"), lax.axis_size("gz")
    if depth_steps == 0:
        return lax.ppermute(value, "ta", [(i, (i + time_steps) % times) for i in range(times)])
    pairs = [
        (t * depths + g, (t + time_steps) % times * depths + (g + depth_steps) % depths)
        for t in range(times)
        for g in range(depths)
    ]
    return lax.ppermute(value, ("ta", "gz"), pairs)


def exchanged(value, axis, odd):
    count = lax.axis_size(axis)
    pairs = [(i, (i + (1 if i % 2 == odd else -1)) % count) for i in range(count)]
    return lax.ppermute(value, axis, pairs)


def exchange_faces(t0, t1, z0, z1):
    z0 = exchanged(z0, "gz", 0)
    t0 = exchanged(t0, "ta", 0)
    z1 = exchanged(z1, "gz", 1)
    t1 = exchanged(t1, "ta", 1)
    return [t0, t1, z0, z1]


def per_device(links, source):
    links = links.reshape((72, 8, 256))
    source = source.reshape((24, 8, 256))
    spinor, half, quarter, rows = (24,) + TILE, (12,) + TILE, (6,) + TILE, (12, 128)
    faces = [rows] * 2 + [half] * 2
    (packed,) = call(pack_links_kernel, [(72,) + TILE], [links])
    moved = moved_to(packed, 1, 0)

    w0, rho0, other, *sent = call(kernel_one, [spinor] * 3 + faces, [links, source], solver=True)
    came = exchange_faces(*sent)
    w1, rest, rho1, send, tb, z0, z1 = call(
        kernel_two,
        [spinor] * 3 + [(36,) + TILE, rows, quarter, quarter],
        [links, rho0, other] + came,
        solver=True,
    )
    z0 = exchanged(z0, "gz", 0)
    z1 = exchanged(z1, "gz", 1)
    send = moved_to(send, 1, 0)
    x0, rho0, other, *sent = call(
        kernel_three,
        [spinor] * 3 + faces,
        [links, moved, rest, rho1, tb, send, z0, z1],
        solver=True,
        moved=True,
    )
    came = exchange_faces(*sent)
    x1, rest, rho1, send, ta, z0, z1, za, zb = call(
        kernel_four,
        [spinor] * 3 + [(48,) + TILE, rows] + [quarter] * 4,
        [links, moved, x0, rho0, other] + came,
        solver=True,
        moved=True,
    )
    z0 = exchanged(z0, "gz", 0)
    z1 = exchanged(z1, "gz", 1)
    send = moved_to(send, -1, 0)
    za = moved_to(za, -1, 1)
    zb = moved_to(zb, -1, -1)
    solution, residual = call(
        kernel_five,
        [(24, 8, 256)] * 2,
        [links, w0, w1, x0, x1, rest, rho1, ta, send, z0, z1, za, zb],
    )
    return solution.reshape((24, 1, 8, 256)), residual.reshape((24, 1, 8, 256))


def solution(mesh):
    in_specs = (P(None, None, "gz", "ta", None), P(None, "gz", "ta", None))
    out_specs = (P(None, "gz", "ta", None), P(None, "gz", "ta", None))
    return jax.shard_map(
        per_device, mesh=mesh, in_specs=in_specs, out_specs=out_specs, check_vma=False
    )
```

profile of v0, /device:TPU:1, one launch (start us, length us, event | category | flops | bytes accessed | tf_op | source)
XLA Modules:
  0.0 61.3 jit_solution(3273249741223993318)
XLA Ops:
  0.6 1.1 %copy-done = f32[4,18,1,8,256]{4,3,2,1,0:T(8,128)S(1)} copy-done((f32[4,18,1,8,256]{4,3,2,1,0:T(8,128)S(1)}, f32[4,18,1,8,256]{4,3,2,1,0:T(8,128)}, u32[]{:S(2)}) %copy-start) | copy-done | bytes 589848
  1.7 0.1 shard_map.43
  1.8 3.1 %collective-permute-start.4 = (f32[72,8,128]{2,1,0:T(8,128)S(1)}, f32[72,8,128]{2,1,0:T(8,128)S(1)}, u32[]{:S(2)}, u32[]{:S(2)}) collective-permute-start(f32[72,8,128]{2,1,0:T(8,128)S(1)} %shard_map.43), channel_id=1, source_target_pairs={{0,4},{4,8},{8,12},{12,16},{16,20},{20,24},{24,28},{28,32},{32,36}... | collective-permute-start | bytes 884744 | tf_op jit(solution)/shard_map/ppermute | solution.py:553
  4.9 1.6 %shard_map.41 = (f32[24,8,128]{2,1,0:T(8,128)S(1)}, f32[24,8,128]{2,1,0:T(8,128)S(1)}, f32[24,8,128]{2,1,0:T(8,128)S(1)}, f32[12,128]{1,0:T(8,128)S(1)}, f32[12,...) custom-call(f32[72,8,256]{2,1,0:T(8,128)S(1)} %bitcast.9, f32[24,8,256]{2,1,0:T(8,128)S(1)} %bitcast.14), custom_call_target="tpu_custom_call" | custom-call | flops 3000000 | bytes 1500000 | tf_op jit(solution)/shard_map/pallas_call | solution.py:539
  6.5 3.1 %collective-permute-start.2 = (f32[12,8,128]{2,1,0:T(8,128)S(1)}, f32[12,8,128]{2,1,0:T(8,128)S(1)}, u32[]{:S(2)}, u32[]{:S(2)}) collective-permute-start(f32[12,8,128]{2,1,0:T(8,128)S(1)} %get-tuple-element.39), channel_id=1, source_target_pairs={{0,1},{1,0},{2,3},{3,2},{4,5},{5,4},{6,7},{7,6},{8,9},{9,8},{10,11... | collective-permute-start | bytes 147464 | tf_op jit(solution)/shard_map/ppermute | solution.py:565
  9.6 3.3 %collective-permute-start.3 = (f32[12,8,128]{2,1,0:T(8,128)S(1)}, f32[12,8,128]{2,1,0:T(8,128)S(1)}, u32[]{:S(2)}, u32[]{:S(2)}) collective-permute-start(f32[12,8,128]{2,1,0:T(8,128)S(1)} %get-tuple-element.40), channel_id=1, source_target_pairs={{0,3},{1,2},{2,1},{3,0},{4,7},{5,6},{6,5},{7,4},{8,11},{9,10},{10,... | collective-permute-start | bytes 147464 | tf_op jit(solution)/shard_map/ppermute | solution.py:565
  12.9 0.7 %collective-permute-start = (f32[12,128]{1,0:T(8,128)S(1)}, f32[12,128]{1,0:T(8,128)S(1)}, u32[]{:S(2)}, u32[]{:S(2)}) collective-permute-start(f32[12,128]{1,0:T(8,128)S(1)} %get-tuple-element.37), channel_id=1, source_target_pairs={{0,4},{4,0},{8,12},{12,8},{16,20},{20,16},{24,28},{28,24},{32,36},... | collective-permute-start | bytes 18440 | tf_op jit(solution)/shard_map/ppermute | solution.py:565
  13.6 1.4 %collective-permute-start.1 = (f32[12,128]{1,0:T(8,128)S(1)}, f32[12,128]{1,0:T(8,128)S(1)}, u32[]{:S(2)}, u32[]{:S(2)}) collective-permute-start(f32[12,128]{1,0:T(8,128)S(1)} %get-tuple-element.38), channel_id=1, source_target_pairs={{0,252},{4,8},{8,4},{12,16},{16,12},{20,24},{24,20},{28,32},{32,28... | collective-permute-start | bytes 18440 | tf_op jit(solution)/shard_map/ppermute | solution.py:565
  15.0 1.7 %collective-permute-done.1.t1_in = f32[12,128]{1,0:T(8,128)S(1)} collective-permute-done((f32[12,128]{1,0:T(8,128)S(1)}, f32[12,128]{1,0:T(8,128)S(1)}, u32[]{:S(2)}, u32[]{:S(2)}) %collective-permute-start.1) | collective-permute-done | bytes 6176 | tf_op jit(solution)/shard_map/ppermute | solution.py:565
  16.7 0.0 collective-permute-done.2.z0_in
  16.7 0.0 collective-permute-done.3.z1_in
  16.7 1.7 %shard_map.42 = (f32[24,8,128]{2,1,0:T(8,128)S(1)}, f32[24,8,128]{2,1,0:T(8,128)S(1)}, f32[24,8,128]{2,1,0:T(8,128)S(1)}, f32[36,8,128]{2,1,0:T(8,128)S(1)}, f32...) custom-call(f32[72,8,256]{2,1,0:T(8,128)S(1)} %bitcast.10, ...), custom_call_target="tpu_custom_call" | custom-call | flops 3000000 | bytes 1500000 | tf_op jit(solution)/shard_map/pallas_call | solution.py:539
  18.4 1.5 %collective-permute-start.5 = (f32[36,8,128]{2,1,0:T(8,128)S(1)}, f32[36,8,128]{2,1,0:T(8,128)S(1)}, u32[]{:S(2)}, u32[]{:S(2)}) collective-permute-start(f32[36,8,128]{2,1,0:T(8,128)S(1)} %get-tuple-element.45), channel_id=1, source_target_pairs={{0,4},{4,8},{8,12},{12,16},{16,20},{20,24},{24,28},{28,32},{32,36}... | collective-permute-start | bytes 442376 | tf_op jit(solution)/shard_map/ppermute | solution.py:553
  19.8 1.2 %collective-permute-start.6 = (f32[6,8,128]{2,1,0:T(8,128)S(1)}, f32[6,8,128]{2,1,0:T(8,128)S(1)}, u32[]{:S(2)}, u32[]{:S(2)}) collective-permute-start(f32[6,8,128]{2,1,0:T(8,128)S(1)} %get-tuple-element.46), channel_id=1, source_target_pairs={{0,1},{1,0},{2,3},{3,2},{4,5},{5,4},{6,7},{7,6},{8,9},{9,8},{10,11... | collective-permute-start | bytes 73736 | tf_op jit(solution)/shard_map/ppermute | solution.py:565
  21.0 3.1 %collective-permute-start.7 = (f32[6,8,128]{2,1,0:T(8,128)S(1)}, f32[6,8,128]{2,1,0:T(8,128)S(1)}, u32[]{:S(2)}, u32[]{:S(2)}) collective-permute-start(f32[6,8,128]{2,1,0:T(8,128)S(1)} %get-tuple-element.47), channel_id=1, source_target_pairs={{0,3},{1,2},{2,1},{3,0},{4,7},{5,6},{6,5},{7,4},{8,11},{9,10},{10,... | collective-permute-start | bytes 73736 | tf_op jit(solution)/shard_map/ppermute | solution.py:565
  24.2 1.8 %collective-permute-done.7.z1_in = f32[6,8,128]{2,1,0:T(8,128)S(1)} collective-permute-done((f32[6,8,128]{2,1,0:T(8,128)S(1)}, f32[6,8,128]{2,1,0:T(8,128)S(1)}, u32[]{:S(2)}, u32[]{:S(2)}) %collective-permute-start.7) | collective-permute-done | bytes 24608 | tf_op jit(solution)/shard_map/ppermute | solution.py:565
  26.0 0.0 collective-permute-done.5.received
  26.0 0.0 collective-permute-done.4.moved_in
  26.0 1.8 %shard_map.44 = (f32[24,8,128]{2,1,0:T(8,128)S(1)}, f32[24,8,128]{2,1,0:T(8,128)S(1)}, f32[24,8,128]{2,1,0:T(8,128)S(1)}, f32[12,128]{1,0:T(8,128)S(1)}, f32[12,...) custom-call(f32[72,8,256]{2,1,0:T(8,128)S(1)} %bitcast.11, ...), custom_call_target="tpu_custom_call" | custom-call | flops 3000000 | bytes 1500000 | tf_op jit(solution)/shard_map/pallas_call | solution.py:539
  27.8 1.1 %collective-permute-start.10 = (f32[12,8,128]{2,1,0:T(8,128)S(1)}, f32[12,8,128]{2,1,0:T(8,128)S(1)}, u32[]{:S(2)}, u32[]{:S(2)}) collective-permute-start(f32[12,8,128]{2,1,0:T(8,128)S(1)} %get-tuple-element.53), channel_id=1, source_target_pairs={{0,1},{1,0},{2,3},{3,2},{4,5},{5,4},{6,7},{7,6},{8,9},{9,8},{10,11... | collective-permute-start | bytes 147464 | tf_op jit(solution)/shard_map/ppermute | solution.py:565
  28.9 2.6 %collective-permute-start.11 = (f32[12,8,128]{2,1,0:T(8,128)S(1)}, f32[12,8,128]{2,1,0:T(8,128)S(1)}, u32[]{:S(2)}, u32[]{:S(2)}) collective-permute-start(f32[12,8,128]{2,1,0:T(8,128)S(1)} %get-tuple-element.54), channel_id=1, source_target_pairs={{0,3},{1,2},{2,1},{3,0},{4,7},{5,6},{6,5},{7,4},{8,11},{9,10},{10,... | collective-permute-start | bytes 147464 | tf_op jit(solution)/shard_map/ppermute | solution.py:565
  31.5 4.1 %collective-permute-start.8 = (f32[12,128]{1,0:T(8,128)S(1)}, f32[12,128]{1,0:T(8,128)S(1)}, u32[]{:S(2)}, u32[]{:S(2)}) collective-permute-start(f32[12,128]{1,0:T(8,128)S(1)} %get-tuple-element.51), channel_id=1, source_target_pairs={{0,4},{4,0},{8,12},{12,8},{16,20},{20,16},{24,28},{28,24},{32,36},... | collective-permute-start | bytes 18440 | tf_op jit(solution)/shard_map/ppermute | solution.py:565
  35.6 0.8 %collective-permute-done.8.t0_in = f32[12,128]{1,0:T(8,128)S(1)} collective-permute-done((f32[12,128]{1,0:T(8,128)S(1)}, f32[12,128]{1,0:T(8,128)S(1)}, u32[]{:S(2)}, u32[]{:S(2)}) %collective-permute-start.8) | collective-permute-done | bytes 6176 | tf_op jit(solution)/shard_map/ppermute | solution.py:565
  36.4 2.2 %collective-permute-done.9.t1_in = f32[12,128]{1,0:T(8,128)S(1)} collective-permute-done((f32[12,128]{1,0:T(8,128)S(1)}, f32[12,128]{1,0:T(8,128)S(1)}, u32[]{:S(2)}, u32[]{:S(2)}) %collective-permute-start.9) | collective-permute-done | bytes 6176 | tf_op jit(solution)/shard_map/ppermute | solution.py:565
  38.7 1.7 %shard_map.45 = (f32[24,8,128]{2,1,0:T(8,128)S(1)}, f32[24,8,128]{2,1,0:T(8,128)S(1)}, f32[24,8,128]{2,1,0:T(8,128)S(1)}, f32[48,8,128]{2,1,0:T(8,128)S(1)}, f32...) custom-call(f32[72,8,256]{2,1,0:T(8,128)S(1)} %bitcast.12, ...), custom_call_target="tpu_custom_call" | custom-call | flops 3000000 | bytes 1500000 | tf_op jit(solution)/shard_map/pallas_call | solution.py:539
  40.4 4.3 %collective-permute-start.12 = (f32[48,8,128]{2,1,0:T(8,128)S(1)}, f32[48,8,128]{2,1,0:T(8,128)S(1)}, u32[]{:S(2)}, u32[]{:S(2)}) collective-permute-start(f32[48,8,128]{2,1,0:T(8,128)S(1)} %get-tuple-element.59), channel_id=1, source_target_pairs={{0,252},{4,0},{8,4},{12,8},{16,12},{20,16},{24,20},{28,24},{32,28}... | collective-permute-start | bytes 589832 | tf_op jit(solution)/shard_map/ppermute | solution.py:553
  44.7 0.9 %collective-permute-start.13 = (f32[6,8,128]{2,1,0:T(8,128)S(1)}, f32[6,8,128]{2,1,0:T(8,128)S(1)}, u32[]{:S(2)}, u32[]{:S(2)}) collective-permute-start(f32[6,8,128]{2,1,0:T(8,128)S(1)} %get-tuple-element.60), channel_id=1, source_target_pairs={{0,1},{1,0},{2,3},{3,2},{4,5},{5,4},{6,7},{7,6},{8,9},{9,8},{10,11... | collective-permute-start | bytes 73736 | tf_op jit(solution)/shard_map/ppermute | solution.py:565
  45.6 3.4 %collective-permute-start.14 = (f32[6,8,128]{2,1,0:T(8,128)S(1)}, f32[6,8,128]{2,1,0:T(8,128)S(1)}, u32[]{:S(2)}, u32[]{:S(2)}) collective-permute-start(f32[6,8,128]{2,1,0:T(8,128)S(1)} %get-tuple-element.61), channel_id=1, source_target_pairs={{0,3},{1,2},{2,1},{3,0},{4,7},{5,6},{6,5},{7,4},{8,11},{9,10},{10,... | collective-permute-start | bytes 73736 | tf_op jit(solution)/shard_map/ppermute | solution.py:565
  49.0 6.4 %collective-permute-start.15 = (f32[6,8,128]{2,1,0:T(8,128)S(1)}, f32[6,8,128]{2,1,0:T(8,128)S(1)}, u32[]{:S(2)}, u32[]{:S(2)}) collective-permute-start(f32[6,8,128]{2,1,0:T(8,128)S(1)} %get-tuple-element.62), channel_id=1, source_target_pairs={{0,253},{1,254},{2,255},{3,252},{4,1},{5,2},{6,3},{7,0},{8,5},{9,6... | collective-permute-start | bytes 73736 | tf_op jit(solution)/shard_map/ppermute | solution.py:559
  55.5 1.7 %collective-permute-start.16 = (f32[6,8,128]{2,1,0:T(8,128)S(1)}, f32[6,8,128]{2,1,0:T(8,128)S(1)}, u32[]{:S(2)}, u32[]{:S(2)}) collective-permute-start(f32[6,8,128]{2,1,0:T(8,128)S(1)} %get-tuple-element.63), channel_id=1, source_target_pairs={{0,255},{1,252},{2,253},{3,254},{4,3},{5,0},{6,1},{7,2},{8,7},{9,4... | collective-permute-start | bytes 73736 | tf_op jit(solution)/shard_map/ppermute | solution.py:559
  57.1 3.4 %collective-permute-done.16.zb_in = f32[6,8,128]{2,1,0:T(8,128)S(1)} collective-permute-done((f32[6,8,128]{2,1,0:T(8,128)S(1)}, f32[6,8,128]{2,1,0:T(8,128)S(1)}, u32[]{:S(2)}, u32[]{:S(2)}) %collective-permute-start.16) | collective-permute-done | bytes 24608 | tf_op jit(solution)/shard_map/ppermute | solution.py:559
  60.5 0.8 %shard_map.46 = (f32[24,8,256]{2,1,0:T(8,128)}, f32[24,8,256]{2,1,0:T(8,128)}) custom-call(f32[72,8,256]{2,1,0:T(8,128)S(1)} %bitcast.13, f32[24,8,128]{2,1,0:T(8,128)S(1)} %get-tuple-element.34.w0_ref, f32[24,8,128]{2,1,0:T(8,128)S(1)} %get-tuple-element.41.w1_ref, f32[24,8,128]{2,1,0:T(8,128)S(1)} %get-tuple-element.48.w_in.x0_ref, ...), custom_call_target="tpu_custom_call" | custom-call | flops 3000000 | bytes 1500000 | tf_op jit(solution)/shard_map/pallas_call | solution.py:539
  (12 shorter events, 0.0 us)
Async XLA Ops:
  0.6 1.1 %copy-start = (f32[4,18,1,8,256]{4,3,2,1,0:T(8,128)S(1)}, f32[4,18,1,8,256]{4,3,2,1,0:T(8,128)}, u32[]{:S(2)}) copy-start(f32[4,18,1,8,256]{4,3,2,1,0:T(8,128)} %param.2) | copy-start | bytes 1769476
  1.7 3.2 %copy-start.1 = (f32[24,1,8,256]{3,2,1,0:T(8,128)S(1)}, f32[24,1,8,256]{3,2,1,0:T(8,128)}, u32[]{:S(2)}) copy-start(f32[24,1,8,256]{3,2,1,0:T(8,128)} %param.3) | copy-start | bytes 589828
  1.8 24.3 %collective-permute-start.4 = (f32[72,8,128]{2,1,0:T(8,128)S(1)}, f32[72,8,128]{2,1,0:T(8,128)S(1)}, u32[]{:S(2)}, u32[]{:S(2)}) collective-permute-start(f32[72,8,128]{2,1,0:T(8,128)S(1)} %shard_map.43), channel_id=1, source_target_pairs={{0,4},{4,8},{8,12},{12,16},{16,20},{20,24},{24,28},{28,32},{32,36}... | collective-permute-start | bytes 884744 | tf_op jit(solution)/shard_map/ppermute | solution.py:553
  6.5 10.2 %collective-permute-start.2 = (f32[12,8,128]{2,1,0:T(8,128)S(1)}, f32[12,8,128]{2,1,0:T(8,128)S(1)}, u32[]{:S(2)}, u32[]{:S(2)}) collective-permute-start(f32[12,8,128]{2,1,0:T(8,128)S(1)} %get-tuple-element.39), channel_id=1, source_target_pairs={{0,1},{1,0},{2,3},{3,2},{4,5},{5,4},{6,7},{7,6},{8,9},{9,8},{10,11... | collective-permute-start | bytes 147464 | tf_op jit(solution)/shard_map/ppermute | solution.py:565
  9.6 7.1 %collective-permute-start.3 = (f32[12,8,128]{2,1,0:T(8,128)S(1)}, f32[12,8,128]{2,1,0:T(8,128)S(1)}, u32[]{:S(2)}, u32[]{:S(2)}) collective-permute-start(f32[12,8,128]{2,1,0:T(8,128)S(1)} %get-tuple-element.40), channel_id=1, source_target_pairs={{0,3},{1,2},{2,1},{3,0},{4,7},{5,6},{6,5},{7,4},{8,11},{9,10},{10,... | collective-permute-start | bytes 147464 | tf_op jit(solution)/shard_map/ppermute | solution.py:565
  12.9 2.1 %collective-permute-start = (f32[12,128]{1,0:T(8,128)S(1)}, f32[12,128]{1,0:T(8,128)S(1)}, u32[]{:S(2)}, u32[]{:S(2)}) collective-permute-start(f32[12,128]{1,0:T(8,128)S(1)} %get-tuple-element.37), channel_id=1, source_target_pairs={{0,4},{4,0},{8,12},{12,8},{16,20},{20,16},{24,28},{28,24},{32,36},... | collective-permute-start | bytes 18440 | tf_op jit(solution)/shard_map/ppermute | solution.py:565
  13.6 3.1 %collective-permute-start.1 = (f32[12,128]{1,0:T(8,128)S(1)}, f32[12,128]{1,0:T(8,128)S(1)}, u32[]{:S(2)}, u32[]{:S(2)}) collective-permute-start(f32[12,128]{1,0:T(8,128)S(1)} %get-tuple-element.38), channel_id=1, source_target_pairs={{0,252},{4,8},{8,4},{12,16},{16,12},{20,24},{24,20},{28,32},{32,28... | collective-permute-start | bytes 18440 | tf_op jit(solution)/shard_map/ppermute | solution.py:565
  18.4 7.7 %collective-permute-start.5 = (f32[36,8,128]{2,1,0:T(8,128)S(1)}, f32[36,8,128]{2,1,0:T(8,128)S(1)}, u32[]{:S(2)}, u32[]{:S(2)}) collective-permute-start(f32[36,8,128]{2,1,0:T(8,128)S(1)} %get-tuple-element.45), channel_id=1, source_target_pairs={{0,4},{4,8},{8,12},{12,16},{16,20},{20,24},{24,28},{28,32},{32,36}... | collective-permute-start | bytes 442376 | tf_op jit(solution)/shard_map/ppermute | solution.py:553
  19.8 4.3 %collective-permute-start.6 = (f32[6,8,128]{2,1,0:T(8,128)S(1)}, f32[6,8,128]{2,1,0:T(8,128)S(1)}, u32[]{:S(2)}, u32[]{:S(2)}) collective-permute-start(f32[6,8,128]{2,1,0:T(8,128)S(1)} %get-tuple-element.46), channel_id=1, source_target_pairs={{0,1},{1,0},{2,3},{3,2},{4,5},{5,4},{6,7},{7,6},{8,9},{9,8},{10,11... | collective-permute-start | bytes 73736 | tf_op jit(solution)/shard_map/ppermute | solution.py:565
  21.0 5.0 %collective-permute-start.7 = (f32[6,8,128]{2,1,0:T(8,128)S(1)}, f32[6,8,128]{2,1,0:T(8,128)S(1)}, u32[]{:S(2)}, u32[]{:S(2)}) collective-permute-start(f32[6,8,128]{2,1,0:T(8,128)S(1)} %get-tuple-element.47), channel_id=1, source_target_pairs={{0,3},{1,2},{2,1},{3,0},{4,7},{5,6},{6,5},{7,4},{8,11},{9,10},{10,... | collective-permute-start | bytes 73736 | tf_op jit(solution)/shard_map/ppermute | solution.py:565
  27.8 10.9 %collective-permute-start.10 = (f32[12,8,128]{2,1,0:T(8,128)S(1)}, f32[12,8,128]{2,1,0:T(8,128)S(1)}, u32[]{:S(2)}, u32[]{:S(2)}) collective-permute-start(f32[12,8,128]{2,1,0:T(8,128)S(1)} %get-tuple-element.53), channel_id=1, source_target_pairs={{0,1},{1,0},{2,3},{3,2},{4,5},{5,4},{6,7},{7,6},{8,9},{9,8},{10,11... | collective-permute-start | bytes 147464 | tf_op jit(solution)/shard_map/ppermute | solution.py:565
  28.9 9.8 %collective-permute-start.11 = (f32[12,8,128]{2,1,0:T(8,128)S(1)}, f32[12,8,128]{2,1,0:T(8,128)S(1)}, u32[]{:S(2)}, u32[]{:S(2)}) collective-permute-start(f32[12,8,128]{2,1,0:T(8,128)S(1)} %get-tuple-element.54), channel_id=1, source_target_pairs={{0,3},{1,2},{2,1},{3,0},{4,7},{5,6},{6,5},{7,4},{8,11},{9,10},{10,... | collective-permute-start | bytes 147464 | tf_op jit(solution)/shard_map/ppermute | solution.py:565
  31.5 4.9 %collective-permute-start.8 = (f32[12,128]{1,0:T(8,128)S(1)}, f32[12,128]{1,0:T(8,128)S(1)}, u32[]{:S(2)}, u32[]{:S(2)}) collective-permute-start(f32[12,128]{1,0:T(8,128)S(1)} %get-tuple-element.51), channel_id=1, source_target_pairs={{0,4},{4,0},{8,12},{12,8},{16,20},{20,16},{24,28},{28,24},{32,36},... | collective-permute-start | bytes 18440 | tf_op jit(solution)/shard_map/ppermute | solution.py:565
  35.6 3.1 %collective-permute-start.9 = (f32[12,128]{1,0:T(8,128)S(1)}, f32[12,128]{1,0:T(8,128)S(1)}, u32[]{:S(2)}, u32[]{:S(2)}) collective-permute-start(f32[12,128]{1,0:T(8,128)S(1)} %get-tuple-element.52), channel_id=1, source_target_pairs={{0,252},{4,8},{8,4},{12,16},{16,12},{20,24},{24,20},{28,32},{32,28... | collective-permute-start | bytes 18440 | tf_op jit(solution)/shard_map/ppermute | solution.py:565
  40.4 20.1 %collective-permute-start.12 = (f32[48,8,128]{2,1,0:T(8,128)S(1)}, f32[48,8,128]{2,1,0:T(8,128)S(1)}, u32[]{:S(2)}, u32[]{:S(2)}) collective-permute-start(f32[48,8,128]{2,1,0:T(8,128)S(1)} %get-tuple-element.59), channel_id=1, source_target_pairs={{0,252},{4,0},{8,4},{12,8},{16,12},{20,16},{24,20},{28,24},{32,28}... | collective-permute-start | bytes 589832 | tf_op jit(solution)/shard_map/ppermute | solution.py:553
  44.7 12.4 %collective-permute-start.13 = (f32[6,8,128]{2,1,0:T(8,128)S(1)}, f32[6,8,128]{2,1,0:T(8,128)S(1)}, u32[]{:S(2)}, u32[]{:S(2)}) collective-permute-start(f32[6,8,128]{2,1,0:T(8,128)S(1)} %get-tuple-element.60), channel_id=1, source_target_pairs={{0,1},{1,0},{2,3},{3,2},{4,5},{5,4},{6,7},{7,6},{8,9},{9,8},{10,11... | collective-permute-start | bytes 73736 | tf_op jit(solution)/shard_map/ppermute | solution.py:565
  45.6 11.5 %collective-permute-start.14 = (f32[6,8,128]{2,1,0:T(8,128)S(1)}, f32[6,8,128]{2,1,0:T(8,128)S(1)}, u32[]{:S(2)}, u32[]{:S(2)}) collective-permute-start(f32[6,8,128]{2,1,0:T(8,128)S(1)} %get-tuple-element.61), channel_id=1, source_target_pairs={{0,3},{1,2},{2,1},{3,0},{4,7},{5,6},{6,5},{7,4},{8,11},{9,10},{10,... | collective-permute-start | bytes 73736 | tf_op jit(solution)/shard_map/ppermute | solution.py:565
  49.0 8.1 %collective-permute-start.15 = (f32[6,8,128]{2,1,0:T(8,128)S(1)}, f32[6,8,128]{2,1,0:T(8,128)S(1)}, u32[]{:S(2)}, u32[]{:S(2)}) collective-permute-start(f32[6,8,128]{2,1,0:T(8,128)S(1)} %get-tuple-element.62), channel_id=1, source_target_pairs={{0,253},{1,254},{2,255},{3,252},{4,1},{5,2},{6,3},{7,0},{8,5},{9,6... | collective-permute-start | bytes 73736 | tf_op jit(solution)/shard_map/ppermute | solution.py:559
  55.5 5.0 %collective-permute-start.16 = (f32[6,8,128]{2,1,0:T(8,128)S(1)}, f32[6,8,128]{2,1,0:T(8,128)S(1)}, u32[]{:S(2)}, u32[]{:S(2)}) collective-permute-start(f32[6,8,128]{2,1,0:T(8,128)S(1)} %get-tuple-element.63), channel_id=1, source_target_pairs={{0,255},{1,252},{2,253},{3,254},{4,3},{5,0},{6,1},{7,2},{8,7},{9,4... | collective-permute-start | bytes 73736 | tf_op jit(solution)/shard_map/ppermute | solution.py:559
where the time goes:
time: 61.5 us; the launch traced here: 61.3 us
  starting transfers between devices  41.9 us (68%)
  waiting for transfers between devices  9.98 us (16%)
  Pallas kernels  7.69 us (13%)
  local copies, waits for them, and re-layouts  1.06 us (2%)
  between operations  0.68 us (1%)
    ppermute x12, starting transfers between devices, exchanged(): return lax.ppermute(value, axis, pairs)  24.9 us
    ppermute x3, starting transfers between devices, moved_to(): lax.ppermute(value, 'ta', [(i, (i + time_steps) % times) for i in range(t...  8.88 us
    ppermute x2, starting transfers between devices, moved_to(): return lax.ppermute(value, ('ta', 'gz'), pairs)  8.1 us
    pallas_call x6, Pallas kernels, call(): pl.pallas_call(kernel, out_shape=[jax.ShapeDtypeStruct(shape, F32) for sh...  7.69 us
    ppermute x12, waiting for transfers between devices, exchanged(): return lax.ppermute(value, axis, pairs)  6.59 us
    ppermute x2, waiting for transfers between devices, moved_to(): return lax.ppermute(value, ('ta', 'gz'), pairs)  3.38 us
  transfers between devices with their start and end apart: 17, of which 5 were waited for; matrix products, arithmetic and copies ran while one was open for 0% of the time, Pallas kernels for 5%

commit v1 on v0

--- a/solution.py
+++ b/solution.py
@@ -165,46 +165,73 @@
     }
     left = (lane // 8) % 2 == 0
 
-    def per_block(value):
-        total_left = jnp.sum(jnp.where(left, value, 0.0), axis=(0, 1), keepdims=True)
-        total_right = jnp.sum(jnp.where(left, 0.0, value), axis=(0, 1), keepdims=True)
-        return jnp.where(left, total_left, total_right) / ENTRIES
-
-    def step(_, carry):
-        rho = load_spinor(rho_ref)
-        total = scaled(rho, DIAGONAL)
+    def apply(field):
+        total = scaled(field, DIAGONAL)
         for slot, direction in enumerate((X, Y, T)):
             matrix = load_link(lambda i: masked_ref[slot * 18 + i])
-            half = map_half(ahead[direction], project(rho, direction, -1))
+            half = map_half(ahead[direction], project(field, direction, -1))
             expand_into(total, color_apply(matrix, half, False), direction, -1)
-            half = color_apply(matrix, project(rho, direction, 1), True)
+            half = color_apply(matrix, project(field, direction, 1), True)
             expand_into(total, map_half(behind[direction], half), direction, 1)
-        store_spinor(applied_ref, total)
+        return total
+
+    def weights(applied, rho):
         real, imag, square = None, None, None
         for s in range(4):
             for c in range(3):
-                (ar, ai), (rr, ri) = total[s][c], rho[s][c]
+                (ar, ai), (rr, ri) = applied[s][c], rho[s][c]
                 pr = ar * rr + ai * ri
                 pi = ar * ri - ai * rr
                 ps = ar * ar + ai * ai
                 real = pr if real is None else real + pr
                 imag = pi if imag is None else imag + pi
                 square = ps if square is None else square + ps
-        denominator = per_block(square) + EPSILON
-        weight_real = per_block(real) / denominator
-        weight_imag = per_block(imag) / denominator
+        sums = []
+        for value in (real, imag, square):
+            value = value + times_by(value, 4)
+            value = value + times_by(value, 2)
+            sums.append(value + times_by(value, 1))
+        kind = time % 4
+        rows = jnp.where(kind == 0, sums[0], jnp.where(kind == 1, sums[1], sums[2]))
+        rows = jnp.where(left == (time < 4), rows, 0.0)
+        means = jnp.sum(rows, axis=1, keepdims=True) / ENTRIES
+        means = jnp.broadcast_to(means, TILE)
+        one_on = times_by(means, -1)
+        under = jnp.where(kind == 0, times_by(means, -2), one_on) + EPSILON
+        ratio = means / under
+
+        def at(row):
+            near = jnp.broadcast_to(ratio[row : row + 1, :], TILE)
+            far = jnp.broadcast_to(ratio[row + 4 : row + 5, :], TILE)
+            return jnp.where(left, near, far)
+
+        return at(0), at(1)
+
+    def advance(weight, again):
+        real, imag = weight
         for i in range(12):
             rr, ri = rho_ref[i], rho_ref[12 + i]
             ar, ai = applied_ref[i], applied_ref[12 + i]
-            w_ref[i] = w_ref[i] + (weight_real * rr - weight_imag * ri)
-            w_ref[12 + i] = w_ref[12 + i] + (weight_real * ri + weight_imag * rr)
-            rho_ref[i] = rr - (weight_real * ar - weight_imag * ai)
-            rho_ref[12 + i] = ri - (weight_real * ai + weight_imag * ar)
+            w_ref[i] = w_ref[i] + (real * rr - imag * ri)
+            w_ref[12 + i] = w_ref[12 + i] + (real * ri + imag * rr)
+            rho_ref[i] = rr - (real * ar - imag * ai)
+            rho_ref[12 + i] = ri - (real * ai + imag * ar)
+            if again is not None:
+                br, bi = again[i // 3][i % 3]
+                applied_ref[i] = ar - (real * br - imag * bi)
+                applied_ref[12 + i] = ai - (real * bi + imag * br)
+
+    def step(_, carry):
+        applied = load_spinor(applied_ref)
+        weight = weights(applied, load_spinor(rho_ref))
+        advance(weight, apply(applied))
         return carry
 
     for i in range(24):
         w_ref[i] = jnp.zeros(TILE, F32)
-    lax.fori_loop(0, NMR, step, 0)
+    store_spinor(applied_ref, apply(load_spinor(rho_ref)))
+    lax.fori_loop(0, NMR - 1, step, 0)
+    advance(weights(load_spinor(applied_ref), load_spinor(rho_ref)), None)
 
 
 def add_local_hops(total, half_w, link_to, link_from):
@@ -365,17 +392,17 @@
     ]
 
 
-def pack_links_kernel(links_ref, out_ref):
-    first = row_zero_first()
-    low = time_ids() < 4
-    for i in range(72):
-        zero = compact(links_ref, i, 0, first)
-        one = compact(links_ref, i, 1, first)
-        out_ref[i] = jnp.where(low, times_by(one, 4), zero)
+def packed_upper(ref):
+    low = time_ids() < 4
+    return [jnp.where(low, times_by(ref[i], 4), ref[12 + i]) for i in range(12)]
+
+
+def unpacked_upper(ref, base):
+    return [ref[base + i] for i in range(12)] + [times_by(ref[base + i], 4) for i in range(12)]
 
 
 def kernel_one(links_ref, source_ref, w_ref, rho_ref, other_ref, t0_ref, t1_ref, z0_ref, z1_ref,
-               applied_ref, masked_ref):
+               packed_ref, applied_ref, masked_ref):
     first = row_zero_first()
     link = raw_links(links_ref)
     for i in range(24):
@@ -387,6 +414,13 @@
     total = load_spinor(other_ref)
     add_local_hops(total, half_w, link[1], link[0])
     store_spinor(other_ref, total)
+    low = time_ids() < 4
+    for i in range(72):
+        zero = compact(links_ref, i, 0, first)
+        one = compact(links_ref, i, 1, first)
+        packed_ref[i] = jnp.where(low, times_by(one, 4), zero)
+    for i, tile in enumerate(packed_upper(rho_ref)):
+        packed_ref[72 + i] = tile
 
 
 def kernel_two(links_ref, rho_in, other_in, t0_in, t1_in, z0_in, z1_in,
@@ -406,11 +440,8 @@
     total = load_spinor(rho_in)
     add_local_hops(total, half_w, link[0], link[1])
     store_spinor(rest_ref, total)
-    low = time_ids() < 4
-    for i in range(24):
-        send_ref[i] = jnp.where(low, times_by(rho_ref[i], 4), rest_ref[i])
-    for i in range(12):
-        send_ref[24 + i] = jnp.where(low, times_by(w_ref[i], 4), w_ref[12 + i])
+    for i, tile in enumerate(packed_upper(rho_ref) + packed_upper(w_ref)):
+        send_ref[i] = tile
 
 
 def kernel_three(links_ref, moved_in, rest_in, rho_in, tb_in, received, z0_in, z1_in,
@@ -420,12 +451,11 @@
     link = moved_links(moved_ref)
     time = time_ids()
     low = time < 4
+    ones, zeros = unpacked_upper(received, 0), unpacked_upper(moved_in, 72)
     for i in range(24):
-        other = received[i]
-        rho_ref[i] = jnp.where(low, other, times_by(rest_in[i], 4))
-        other_ref[i] = jnp.where(low, times_by(other, 4), times_by(rho_in[i], 4))
-    came = [jnp.where(low, 0.5 * received[24 + i], 0.0) for i in range(12)]
-    came += [jnp.where(low, 0.5 * times_by(received[24 + i], 4), 0.0) for i in range(12)]
+        rho_ref[i] = jnp.where(low, ones[i], times_by(rest_in[i], 4))
+        other_ref[i] = jnp.where(low, zeros[i], times_by(rho_in[i], 4))
+    came = [jnp.where(low, 0.5 * v, 0.0) for v in unpacked_upper(received, 12)]
     came = [[(came[s * 3 + c], came[12 + s * 3 + c]) for c in range(3)] for s in range(4)]
     total = load_spinor(rho_ref)
     lower, higher = load_pairs(
@@ -449,7 +479,7 @@
     add_spinor(depth_half_w, half_w)
     store_faces(half_w, depth_half_w, link[0], (t0_ref, t1_ref), (z0_ref, z1_ref))
     total = load_spinor(other_ref)
-    add_local_hops(total, half_w, link[1], link[0])
+    add_local_hops(total, depth_half_w, link[1], link[0])
     store_spinor(other_ref, total)
 
 
@@ -578,14 +608,14 @@
     source = source.reshape((24, 8, 256))
     spinor, half, quarter, rows = (24,) + TILE, (12,) + TILE, (6,) + TILE, (12, 128)
     faces = [rows] * 2 + [half] * 2
-    (packed,) = call(pack_links_kernel, [(72,) + TILE], [links])
+    w0, rho0, other, *sent, packed = call(
+        kernel_one, [spinor] * 3 + faces + [(84,) + TILE], [links, source], solver=True
+    )
     moved = moved_to(packed, 1, 0)
-
-    w0, rho0, other, *sent = call(kernel_one, [spinor] * 3 + faces, [links, source], solver=True)
     came = exchange_faces(*sent)
     w1, rest, rho1, send, tb, z0, z1 = call(
         kernel_two,
-        [spinor] * 3 + [(36,) + TILE, rows, quarter, quarter],
+        [spinor] * 3 + [(24,) + TILE, rows, quarter, quarter],
         [links, rho0, other] + came,
         solver=True,
     )

time: 61.5 us -> 59.9 us (0.974)
  starting transfers between devices: 41.9 us -> 38.4 us
  waiting for transfers between devices: 9.98 us -> 12.7 us
  Pallas kernels: 7.69 us -> 5.94 us
  local copies, waits for them, and re-layouts: 1.06 us -> 1.98 us
    ppermute x12, waiting for transfers between devices: 6.59 us -> 9.33 us  [exchanged(): return lax.ppermute(value, axis, pairs)]
    ppermute x12, starting transfers between devices: 24.9 us -> 23 us  [exchanged(): return lax.ppermute(value, axis, pairs)]
    pallas_call x6 -> x5, Pallas kernels: 7.69 us -> 5.94 us  [call(): pl.pallas_call(kernel, out_shape=[jax.ShapeDtypeStruct(shape, F32) for sh...]
    ppermute x3, starting transfers between devices: 8.88 us -> 7.47 us  [moved_to(): lax.ppermute(value, 'ta', [(i, (i + time_steps) % times) for i in range(t...]
    unnamed x4, local copies, waits for them, and re-layouts: 1.06 us -> 1.98 us
  transfers between devices with their start and end apart: 17 -> 17, of which waited for: 5 -> 7; matrix products, arithmetic and copies ran while one was open for 0% -> 0% of each run, Pallas kernels for 5% -> 2%
where the time goes in v1:
time: 59.9 us; the launch traced here: 59.7 us
  starting transfers between devices  38.4 us (64%)
  waiting for transfers between devices  12.7 us (21%)
  Pallas kernels  5.94 us (10%)
  local copies, waits for them, and re-layouts  1.98 us (3%)
  between operations  0.69 us (1%)
    ppermute x12, starting transfers between devices, exchanged(): return lax.ppermute(value, axis, pairs)  23 us
    ppermute x12, waiting for transfers between devices, exchanged(): return lax.ppermute(value, axis, pairs)  9.33 us
    ppermute x2, starting transfers between devices, moved_to(): return lax.ppermute(value, ('ta', 'gz'), pairs)  7.93 us
    ppermute x3, starting transfers between devices, moved_to(): lax.ppermute(value, 'ta', [(i, (i + time_steps) % times) for i in range(t...  7.47 us
    pallas_call x5, Pallas kernels, call(): pl.pallas_call(kernel, out_shape=[jax.ShapeDtypeStruct(shape, F32) for sh...  5.94 us
    ppermute x2, waiting for transfers between devices, moved_to(): return lax.ppermute(value, ('ta', 'gz'), pairs)  3.38 us
    unnamed x4, local copies, waits for them, and re-layouts  1.98 us
  transfers between devices with their start and end apart: 17, of which 7 were waited for; matrix products, arithmetic and copies ran while one was open for 0% of the time, Pallas kernels for 2%

profile of v1, /device:TPU:1, one launch (start us, length us, event | category | flops | bytes accessed | tf_op | source)
XLA Modules:
  0.0 59.7 jit_solution(5554329064120108745)
XLA Ops:
  0.6 1.1 %copy-done = f32[4,18,1,8,256]{4,3,2,1,0:T(8,128)S(1)} copy-done((f32[4,18,1,8,256]{4,3,2,1,0:T(8,128)S(1)}, f32[4,18,1,8,256]{4,3,2,1,0:T(8,128)}, u32[]{:S(2)}) %copy-start) | copy-done | bytes 589848
  1.7 0.9 %copy-done.1 = f32[24,1,8,256]{3,2,1,0:T(8,128)S(1)} copy-done((f32[24,1,8,256]{3,2,1,0:T(8,128)S(1)}, f32[24,1,8,256]{3,2,1,0:T(8,128)}, u32[]{:S(2)}) %copy-start.1) | copy-done | bytes 196632
  2.6 1.2 %shard_map.41 = (f32[24,8,128]{2,1,0:T(8,128)S(1)}, f32[24,8,128]{2,1,0:T(8,128)S(1)}, f32[24,8,128]{2,1,0:T(8,128)S(1)}, f32[12,128]{1,0:T(8,128)S(1)}, f32[12,...) custom-call(f32[72,8,256]{2,1,0:T(8,128)S(1)} %bitcast.8, ...), custom_call_target="tpu_custom_call" | custom-call | flops 3000000 | bytes 1500000 | tf_op jit(solution)/shard_map/pallas_call | solution.py:569
  3.9 3.1 %collective-permute-start.4 = (f32[84,8,128]{2,1,0:T(8,128)S(1)}, f32[84,8,128]{2,1,0:T(8,128)S(1)}, u32[]{:S(2)}, u32[]{:S(2)}) collective-permute-start(f32[84,8,128]{2,1,0:T(8,128)S(1)} %get-tuple-element.43), channel_id=1, source_target_pairs={{0,4},{4,8},{8,12},{12,16},{16,20},{20,24},{24,28},{28,32},{32,36}... | collective-permute-start | bytes 1032200 | tf_op jit(solution)/shard_map/ppermute | solution.py:583
  7.0 3.0 %collective-permute-start.2 = (f32[12,8,128]{2,1,0:T(8,128)S(1)}, f32[12,8,128]{2,1,0:T(8,128)S(1)}, u32[]{:S(2)}, u32[]{:S(2)}) collective-permute-start(f32[12,8,128]{2,1,0:T(8,128)S(1)} %get-tuple-element.40), channel_id=1, source_target_pairs={{0,1},{1,0},{2,3},{3,2},{4,5},{5,4},{6,7},{7,6},{8,9},{9,8},{10,11... | collective-permute-start | bytes 147464 | tf_op jit(solution)/shard_map/ppermute | solution.py:595
  10.0 3.3 %collective-permute-start.3 = (f32[12,8,128]{2,1,0:T(8,128)S(1)}, f32[12,8,128]{2,1,0:T(8,128)S(1)}, u32[]{:S(2)}, u32[]{:S(2)}) collective-permute-start(f32[12,8,128]{2,1,0:T(8,128)S(1)} %get-tuple-element.41), channel_id=1, source_target_pairs={{0,3},{1,2},{2,1},{3,0},{4,7},{5,6},{6,5},{7,4},{8,11},{9,10},{10,... | collective-permute-start | bytes 147464 | tf_op jit(solution)/shard_map/ppermute | solution.py:595
  13.3 0.0 collective-permute-start
  13.3 2.1 %collective-permute-start.1 = (f32[12,128]{1,0:T(8,128)S(1)}, f32[12,128]{1,0:T(8,128)S(1)}, u32[]{:S(2)}, u32[]{:S(2)}) collective-permute-start(f32[12,128]{1,0:T(8,128)S(1)} %get-tuple-element.39), channel_id=1, source_target_pairs={{0,252},{4,8},{8,4},{12,16},{16,12},{20,24},{24,20},{28,32},{32,28... | collective-permute-start | bytes 18440 | tf_op jit(solution)/shard_map/ppermute | solution.py:595
  15.4 0.0 collective-permute-done.t0_in
  15.4 1.6 %collective-permute-done.1.t1_in = f32[12,128]{1,0:T(8,128)S(1)} collective-permute-done((f32[12,128]{1,0:T(8,128)S(1)}, f32[12,128]{1,0:T(8,128)S(1)}, u32[]{:S(2)}, u32[]{:S(2)}) %collective-permute-start.1) | collective-permute-done | bytes 6176 | tf_op jit(solution)/shard_map/ppermute | solution.py:595
  17.0 1.8 %collective-permute-done.3.z1_in = f32[12,8,128]{2,1,0:T(8,128)S(1)} collective-permute-done((f32[12,8,128]{2,1,0:T(8,128)S(1)}, f32[12,8,128]{2,1,0:T(8,128)S(1)}, u32[]{:S(2)}, u32[]{:S(2)}) %collective-permute-start.3) | collective-permute-done | bytes 49184 | tf_op jit(solution)/shard_map/ppermute | solution.py:595
  18.8 1.2 %shard_map.42 = (f32[24,8,128]{2,1,0:T(8,128)S(1)}, f32[24,8,128]{2,1,0:T(8,128)S(1)}, f32[24,8,128]{2,1,0:T(8,128)S(1)}, f32[24,8,128]{2,1,0:T(8,128)S(1)}, f32...) custom-call(f32[72,8,256]{2,1,0:T(8,128)S(1)} %bitcast.9, ...), custom_call_target="tpu_custom_call" | custom-call | flops 3000000 | bytes 1500000 | tf_op jit(solution)/shard_map/pallas_call | solution.py:569
  20.1 0.1 collective-permute-start.5
  20.2 0.8 %collective-permute-start.6 = (f32[6,8,128]{2,1,0:T(8,128)S(1)}, f32[6,8,128]{2,1,0:T(8,128)S(1)}, u32[]{:S(2)}, u32[]{:S(2)}) collective-permute-start(f32[6,8,128]{2,1,0:T(8,128)S(1)} %get-tuple-element.48), channel_id=1, source_target_pairs={{0,1},{1,0},{2,3},{3,2},{4,5},{5,4},{6,7},{7,6},{8,9},{9,8},{10,11... | collective-permute-start | bytes 73736 | tf_op jit(solution)/shard_map/ppermute | solution.py:595
  21.0 2.0 %collective-permute-start.7 = (f32[6,8,128]{2,1,0:T(8,128)S(1)}, f32[6,8,128]{2,1,0:T(8,128)S(1)}, u32[]{:S(2)}, u32[]{:S(2)}) collective-permute-start(f32[6,8,128]{2,1,0:T(8,128)S(1)} %get-tuple-element.49), channel_id=1, source_target_pairs={{0,3},{1,2},{2,1},{3,0},{4,7},{5,6},{6,5},{7,4},{8,11},{9,10},{10,... | collective-permute-start | bytes 73736 | tf_op jit(solution)/shard_map/ppermute | solution.py:595
  23.0 0.9 %collective-permute-done.6.z0_in = f32[6,8,128]{2,1,0:T(8,128)S(1)} collective-permute-done((f32[6,8,128]{2,1,0:T(8,128)S(1)}, f32[6,8,128]{2,1,0:T(8,128)S(1)}, u32[]{:S(2)}, u32[]{:S(2)}) %collective-permute-start.6) | collective-permute-done | bytes 24608 | tf_op jit(solution)/shard_map/ppermute | solution.py:595
  23.8 2.0 %collective-permute-done.7.z1_in = f32[6,8,128]{2,1,0:T(8,128)S(1)} collective-permute-done((f32[6,8,128]{2,1,0:T(8,128)S(1)}, f32[6,8,128]{2,1,0:T(8,128)S(1)}, u32[]{:S(2)}, u32[]{:S(2)}) %collective-permute-start.7) | collective-permute-done | bytes 24608 | tf_op jit(solution)/shard_map/ppermute | solution.py:595
  25.8 0.0 collective-permute-done.4.moved_in
  25.8 1.3 %shard_map.43 = (f32[24,8,128]{2,1,0:T(8,128)S(1)}, f32[24,8,128]{2,1,0:T(8,128)S(1)}, f32[24,8,128]{2,1,0:T(8,128)S(1)}, f32[12,128]{1,0:T(8,128)S(1)}, f32[12,...) custom-call(f32[72,8,256]{2,1,0:T(8,128)S(1)} %bitcast.10, ...), custom_call_target="tpu_custom_call" | custom-call | flops 3000000 | bytes 1500000 | tf_op jit(solution)/shard_map/pallas_call | solution.py:569
  27.1 1.7 %collective-permute-start.10 = (f32[12,8,128]{2,1,0:T(8,128)S(1)}, f32[12,8,128]{2,1,0:T(8,128)S(1)}, u32[]{:S(2)}, u32[]{:S(2)}) collective-permute-start(f32[12,8,128]{2,1,0:T(8,128)S(1)} %get-tuple-element.55), channel_id=1, source_target_pairs={{0,1},{1,0},{2,3},{3,2},{4,5},{5,4},{6,7},{7,6},{8,9},{9,8},{10,11... | collective-permute-start | bytes 147464 | tf_op jit(solution)/shard_map/ppermute | solution.py:595
  28.8 2.1 %collective-permute-start.11 = (f32[12,8,128]{2,1,0:T(8,128)S(1)}, f32[12,8,128]{2,1,0:T(8,128)S(1)}, u32[]{:S(2)}, u32[]{:S(2)}) collective-permute-start(f32[12,8,128]{2,1,0:T(8,128)S(1)} %get-tuple-element.56), channel_id=1, source_target_pairs={{0,3},{1,2},{2,1},{3,0},{4,7},{5,6},{6,5},{7,4},{8,11},{9,10},{10,... | collective-permute-start | bytes 147464 | tf_op jit(solution)/shard_map/ppermute | solution.py:595
  30.9 6.5 %collective-permute-start.8 = (f32[12,128]{1,0:T(8,128)S(1)}, f32[12,128]{1,0:T(8,128)S(1)}, u32[]{:S(2)}, u32[]{:S(2)}) collective-permute-start(f32[12,128]{1,0:T(8,128)S(1)} %get-tuple-element.53), channel_id=1, source_target_pairs={{0,4},{4,0},{8,12},{12,8},{16,20},{20,16},{24,28},{28,24},{32,36},... | collective-permute-start | bytes 18440 | tf_op jit(solution)/shard_map/ppermute | solution.py:595
  37.4 0.8 %collective-permute-done.8.t0_in = f32[12,128]{1,0:T(8,128)S(1)} collective-permute-done((f32[12,128]{1,0:T(8,128)S(1)}, f32[12,128]{1,0:T(8,128)S(1)}, u32[]{:S(2)}, u32[]{:S(2)}) %collective-permute-start.8) | collective-permute-done | bytes 6176 | tf_op jit(solution)/shard_map/ppermute | solution.py:595
  38.2 2.2 %collective-permute-done.9.t1_in = f32[12,128]{1,0:T(8,128)S(1)} collective-permute-done((f32[12,128]{1,0:T(8,128)S(1)}, f32[12,128]{1,0:T(8,128)S(1)}, u32[]{:S(2)}, u32[]{:S(2)}) %collective-permute-start.9) | collective-permute-done | bytes 6176 | tf_op jit(solution)/shard_map/ppermute | solution.py:595
  40.5 1.3 %shard_map.44 = (f32[24,8,128]{2,1,0:T(8,128)S(1)}, f32[24,8,128]{2,1,0:T(8,128)S(1)}, f32[24,8,128]{2,1,0:T(8,128)S(1)}, f32[48,8,128]{2,1,0:T(8,128)S(1)}, f32...) custom-call(f32[72,8,256]{2,1,0:T(8,128)S(1)} %bitcast.11, ...), custom_call_target="tpu_custom_call" | custom-call | flops 3000000 | bytes 1500000 | tf_op jit(solution)/shard_map/pallas_call | solution.py:569
  41.8 4.3 %collective-permute-start.12 = (f32[48,8,128]{2,1,0:T(8,128)S(1)}, f32[48,8,128]{2,1,0:T(8,128)S(1)}, u32[]{:S(2)}, u32[]{:S(2)}) collective-permute-start(f32[48,8,128]{2,1,0:T(8,128)S(1)} %get-tuple-element.61), channel_id=1, source_target_pairs={{0,252},{4,0},{8,4},{12,8},{16,12},{20,16},{24,20},{28,24},{32,28}... | collective-permute-start | bytes 589832 | tf_op jit(solution)/shard_map/ppermute | solution.py:583
  46.1 0.4 collective-permute-start.13
  46.5 1.1 %collective-permute-start.14 = (f32[6,8,128]{2,1,0:T(8,128)S(1)}, f32[6,8,128]{2,1,0:T(8,128)S(1)}, u32[]{:S(2)}, u32[]{:S(2)}) collective-permute-start(f32[6,8,128]{2,1,0:T(8,128)S(1)} %get-tuple-element.63), channel_id=1, source_target_pairs={{0,3},{1,2},{2,1},{3,0},{4,7},{5,6},{6,5},{7,4},{8,11},{9,10},{10,... | collective-permute-start | bytes 73736 | tf_op jit(solution)/shard_map/ppermute | solution.py:595
  47.6 6.3 %collective-permute-start.15 = (f32[6,8,128]{2,1,0:T(8,128)S(1)}, f32[6,8,128]{2,1,0:T(8,128)S(1)}, u32[]{:S(2)}, u32[]{:S(2)}) collective-permute-start(f32[6,8,128]{2,1,0:T(8,128)S(1)} %get-tuple-element.64), channel_id=1, source_target_pairs={{0,253},{1,254},{2,255},{3,252},{4,1},{5,2},{6,3},{7,0},{8,5},{9,6... | collective-permute-start | bytes 73736 | tf_op jit(solution)/shard_map/ppermute | solution.py:589
  53.9 1.7 %collective-permute-start.16 = (f32[6,8,128]{2,1,0:T(8,128)S(1)}, f32[6,8,128]{2,1,0:T(8,128)S(1)}, u32[]{:S(2)}, u32[]{:S(2)}) collective-permute-start(f32[6,8,128]{2,1,0:T(8,128)S(1)} %get-tuple-element.65), channel_id=1, source_target_pairs={{0,255},{1,252},{2,253},{3,254},{4,3},{5,0},{6,1},{7,2},{8,7},{9,4... | collective-permute-start | bytes 73736 | tf_op jit(solution)/shard_map/ppermute | solution.py:589
  55.5 3.4 %collective-permute-done.16.zb_in = f32[6,8,128]{2,1,0:T(8,128)S(1)} collective-permute-done((f32[6,8,128]{2,1,0:T(8,128)S(1)}, f32[6,8,128]{2,1,0:T(8,128)S(1)}, u32[]{:S(2)}, u32[]{:S(2)}) %collective-permute-start.16) | collective-permute-done | bytes 24608 | tf_op jit(solution)/shard_map/ppermute | solution.py:589
  58.9 0.8 %shard_map.45 = (f32[24,8,256]{2,1,0:T(8,128)}, f32[24,8,256]{2,1,0:T(8,128)}) custom-call(f32[72,8,256]{2,1,0:T(8,128)S(1)} %bitcast.12, f32[24,8,128]{2,1,0:T(8,128)S(1)} %get-tuple-element.35.w0_ref, f32[24,8,128]{2,1,0:T(8,128)S(1)} %get-tuple-element.42.w1_ref, f32[24,8,128]{2,1,0:T(8,128)S(1)} %get-tuple-element.50.w_in.x0_ref, ...), custom_call_target="tpu_custom_call" | custom-call | flops 3000000 | bytes 1500000 | tf_op jit(solution)/shard_map/pallas_call | solution.py:569
  (11 shorter events, 0.0 us)
Async XLA Ops:
  0.6 1.1 %copy-start = (f32[4,18,1,8,256]{4,3,2,1,0:T(8,128)S(1)}, f32[4,18,1,8,256]{4,3,2,1,0:T(8,128)}, u32[]{:S(2)}) copy-start(f32[4,18,1,8,256]{4,3,2,1,0:T(8,128)} %param.2) | copy-start | bytes 1769476
  1.7 0.9 %copy-start.1 = (f32[24,1,8,256]{3,2,1,0:T(8,128)S(1)}, f32[24,1,8,256]{3,2,1,0:T(8,128)}, u32[]{:S(2)}) copy-start(f32[24,1,8,256]{3,2,1,0:T(8,128)} %param.3) | copy-start | bytes 589828
  3.9 21.9 %collective-permute-start.4 = (f32[84,8,128]{2,1,0:T(8,128)S(1)}, f32[84,8,128]{2,1,0:T(8,128)S(1)}, u32[]{:S(2)}, u32[]{:S(2)}) collective-permute-start(f32[84,8,128]{2,1,0:T(8,128)S(1)} %get-tuple-element.43), channel_id=1, source_target_pairs={{0,4},{4,8},{8,12},{12,16},{16,20},{20,24},{24,28},{28,32},{32,36}... | collective-permute-start | bytes 1032200 | tf_op jit(solution)/shard_map/ppermute | solution.py:583
  7.0 10.1 %collective-permute-start.2 = (f32[12,8,128]{2,1,0:T(8,128)S(1)}, f32[12,8,128]{2,1,0:T(8,128)S(1)}, u32[]{:S(2)}, u32[]{:S(2)}) collective-permute-start(f32[12,8,128]{2,1,0:T(8,128)S(1)} %get-tuple-element.40), channel_id=1, source_target_pairs={{0,1},{1,0},{2,3},{3,2},{4,5},{5,4},{6,7},{7,6},{8,9},{9,8},{10,11... | collective-permute-start | bytes 147464 | tf_op jit(solution)/shard_map/ppermute | solution.py:595
  10.0 8.9 %collective-permute-start.3 = (f32[12,8,128]{2,1,0:T(8,128)S(1)}, f32[12,8,128]{2,1,0:T(8,128)S(1)}, u32[]{:S(2)}, u32[]{:S(2)}) collective-permute-start(f32[12,8,128]{2,1,0:T(8,128)S(1)} %get-tuple-element.41), channel_id=1, source_target_pairs={{0,3},{1,2},{2,1},{3,0},{4,7},{5,6},{6,5},{7,4},{8,11},{9,10},{10,... | collective-permute-start | bytes 147464 | tf_op jit(solution)/shard_map/ppermute | solution.py:595
  13.3 2.1 %collective-permute-start = (f32[12,128]{1,0:T(8,128)S(1)}, f32[12,128]{1,0:T(8,128)S(1)}, u32[]{:S(2)}, u32[]{:S(2)}) collective-permute-start(f32[12,128]{1,0:T(8,128)S(1)} %get-tuple-element.38), channel_id=1, source_target_pairs={{0,4},{4,0},{8,12},{12,8},{16,20},{20,16},{24,28},{28,24},{32,36},... | collective-permute-start | bytes 18440 | tf_op jit(solution)/shard_map/ppermute | solution.py:595
  13.3 3.7 %collective-permute-start.1 = (f32[12,128]{1,0:T(8,128)S(1)}, f32[12,128]{1,0:T(8,128)S(1)}, u32[]{:S(2)}, u32[]{:S(2)}) collective-permute-start(f32[12,128]{1,0:T(8,128)S(1)} %get-tuple-element.39), channel_id=1, source_target_pairs={{0,252},{4,8},{8,4},{12,16},{16,12},{20,24},{24,20},{28,32},{32,28... | collective-permute-start | bytes 18440 | tf_op jit(solution)/shard_map/ppermute | solution.py:595
  20.1 5.7 %collective-permute-start.5 = (f32[24,8,128]{2,1,0:T(8,128)S(1)}, f32[24,8,128]{2,1,0:T(8,128)S(1)}, u32[]{:S(2)}, u32[]{:S(2)}) collective-permute-start(f32[24,8,128]{2,1,0:T(8,128)S(1)} %get-tuple-element.47), channel_id=1, source_target_pairs={{0,4},{4,8},{8,12},{12,16},{16,20},{20,24},{24,28},{28,32},{32,36}... | collective-permute-start | bytes 294920 | tf_op jit(solution)/shard_map/ppermute | solution.py:583
  20.2 3.7 %collective-permute-start.6 = (f32[6,8,128]{2,1,0:T(8,128)S(1)}, f32[6,8,128]{2,1,0:T(8,128)S(1)}, u32[]{:S(2)}, u32[]{:S(2)}) collective-permute-start(f32[6,8,128]{2,1,0:T(8,128)S(1)} %get-tuple-element.48), channel_id=1, source_target_pairs={{0,1},{1,0},{2,3},{3,2},{4,5},{5,4},{6,7},{7,6},{8,9},{9,8},{10,11... | collective-permute-start | bytes 73736 | tf_op jit(solution)/shard_map/ppermute | solution.py:595
  21.0 4.8 %collective-permute-start.7 = (f32[6,8,128]{2,1,0:T(8,128)S(1)}, f32[6,8,128]{2,1,0:T(8,128)S(1)}, u32[]{:S(2)}, u32[]{:S(2)}) collective-permute-start(f32[6,8,128]{2,1,0:T(8,128)S(1)} %get-tuple-element.49), channel_id=1, source_target_pairs={{0,3},{1,2},{2,1},{3,0},{4,7},{5,6},{6,5},{7,4},{8,11},{9,10},{10,... | collective-permute-start | bytes 73736 | tf_op jit(solution)/shard_map/ppermute | solution.py:595
  27.1 13.3 %collective-permute-start.10 = (f32[12,8,128]{2,1,0:T(8,128)S(1)}, f32[12,8,128]{2,1,0:T(8,128)S(1)}, u32[]{:S(2)}, u32[]{:S(2)}) collective-permute-start(f32[12,8,128]{2,1,0:T(8,128)S(1)} %get-tuple-element.55), channel_id=1, source_target_pairs={{0,1},{1,0},{2,3},{3,2},{4,5},{5,4},{6,7},{7,6},{8,9},{9,8},{10,11... | collective-permute-start | bytes 147464 | tf_op jit(solution)/shard_map/ppermute | solution.py:595
  28.8 11.6 %collective-permute-start.11 = (f32[12,8,128]{2,1,0:T(8,128)S(1)}, f32[12,8,128]{2,1,0:T(8,128)S(1)}, u32[]{:S(2)}, u32[]{:S(2)}) collective-permute-start(f32[12,8,128]{2,1,0:T(8,128)S(1)} %get-tuple-element.56), channel_id=1, source_target_pairs={{0,3},{1,2},{2,1},{3,0},{4,7},{5,6},{6,5},{7,4},{8,11},{9,10},{10,... | collective-permute-start | bytes 147464 | tf_op jit(solution)/shard_map/ppermute | solution.py:595
  30.9 7.3 %collective-permute-start.8 = (f32[12,128]{1,0:T(8,128)S(1)}, f32[12,128]{1,0:T(8,128)S(1)}, u32[]{:S(2)}, u32[]{:S(2)}) collective-permute-start(f32[12,128]{1,0:T(8,128)S(1)} %get-tuple-element.53), channel_id=1, source_target_pairs={{0,4},{4,0},{8,12},{12,8},{16,20},{20,16},{24,28},{28,24},{32,36},... | collective-permute-start | bytes 18440 | tf_op jit(solution)/shard_map/ppermute | solution.py:595
  37.4 3.1 %collective-permute-start.9 = (f32[12,128]{1,0:T(8,128)S(1)}, f32[12,128]{1,0:T(8,128)S(1)}, u32[]{:S(2)}, u32[]{:S(2)}) collective-permute-start(f32[12,128]{1,0:T(8,128)S(1)} %get-tuple-element.54), channel_id=1, source_target_pairs={{0,252},{4,8},{8,4},{12,16},{16,12},{20,24},{24,20},{28,32},{32,28... | collective-permute-start | bytes 18440 | tf_op jit(solution)/shard_map/ppermute | solution.py:595
  41.8 17.1 %collective-permute-start.12 = (f32[48,8,128]{2,1,0:T(8,128)S(1)}, f32[48,8,128]{2,1,0:T(8,128)S(1)}, u32[]{:S(2)}, u32[]{:S(2)}) collective-permute-start(f32[48,8,128]{2,1,0:T(8,128)S(1)} %get-tuple-element.61), channel_id=1, source_target_pairs={{0,252},{4,0},{8,4},{12,8},{16,12},{20,16},{24,20},{28,24},{32,28}... | collective-permute-start | bytes 589832 | tf_op jit(solution)/shard_map/ppermute | solution.py:583
  46.1 9.4 %collective-permute-start.13 = (f32[6,8,128]{2,1,0:T(8,128)S(1)}, f32[6,8,128]{2,1,0:T(8,128)S(1)}, u32[]{:S(2)}, u32[]{:S(2)}) collective-permute-start(f32[6,8,128]{2,1,0:T(8,128)S(1)} %get-tuple-element.62), channel_id=1, source_target_pairs={{0,1},{1,0},{2,3},{3,2},{4,5},{5,4},{6,7},{7,6},{8,9},{9,8},{10,11... | collective-permute-start | bytes 73736 | tf_op jit(solution)/shard_map/ppermute | solution.py:595
  46.5 9.0 %collective-permute-start.14 = (f32[6,8,128]{2,1,0:T(8,128)S(1)}, f32[6,8,128]{2,1,0:T(8,128)S(1)}, u32[]{:S(2)}, u32[]{:S(2)}) collective-permute-start(f32[6,8,128]{2,1,0:T(8,128)S(1)} %get-tuple-element.63), channel_id=1, source_target_pairs={{0,3},{1,2},{2,1},{3,0},{4,7},{5,6},{6,5},{7,4},{8,11},{9,10},{10,... | collective-permute-start | bytes 73736 | tf_op jit(solution)/shard_map/ppermute | solution.py:595
  47.6 7.9 %collective-permute-start.15 = (f32[6,8,128]{2,1,0:T(8,128)S(1)}, f32[6,8,128]{2,1,0:T(8,128)S(1)}, u32[]{:S(2)}, u32[]{:S(2)}) collective-permute-start(f32[6,8,128]{2,1,0:T(8,128)S(1)} %get-tuple-element.64), channel_id=1, source_target_pairs={{0,253},{1,254},{2,255},{3,252},{4,1},{5,2},{6,3},{7,0},{8,5},{9,6... | collective-permute-start | bytes 73736 | tf_op jit(solution)/shard_map/ppermute | solution.py:589
  53.9 5.0 %collective-permute-start.16 = (f32[6,8,128]{2,1,0:T(8,128)S(1)}, f32[6,8,128]{2,1,0:T(8,128)S(1)}, u32[]{:S(2)}, u32[]{:S(2)}) collective-permute-start(f32[6,8,128]{2,1,0:T(8,128)S(1)} %get-tuple-element.65), channel_id=1, source_target_pairs={{0,255},{1,252},{2,253},{3,254},{4,3},{5,0},{6,1},{7,2},{8,7},{9,4... | collective-permute-start | bytes 73736 | tf_op jit(solution)/shard_map/ppermute | solution.py:589

commit v2 on v1

--- a/solution.py
+++ b/solution.py
@@ -401,14 +401,30 @@
     return [ref[base + i] for i in range(12)] + [times_by(ref[base + i], 4) for i in range(12)]
 
 
-def kernel_one(links_ref, source_ref, w_ref, rho_ref, other_ref, t0_ref, t1_ref, z0_ref, z1_ref,
-               packed_ref, applied_ref, masked_ref):
+def kernel_one(links_hbm, source_hbm, w_ref, rho_ref, other_ref, t0_ref, t1_ref, z0_ref, z1_ref,
+               packed_ref, links_ref, applied_ref, masked_ref, source_ref, arrived):
     first = row_zero_first()
     link = raw_links(links_ref)
+    copies = [
+        pltpu.make_async_copy(
+            links_hbm.at[direction * 18 : direction * 18 + 18],
+            links_ref.at[direction * 18 : direction * 18 + 18],
+            arrived.at[direction],
+        )
+        for direction in range(4)
+    ]
+    source_copy = pltpu.make_async_copy(source_hbm, source_ref, arrived.at[4])
+    source_copy.start()
+    for direction in (X, Y, T, Z):
+        copies[direction].start()
+    source_copy.wait()
     for i in range(24):
         rho_ref[i] = compact(source_ref, i, 0, first)
         other_ref[i] = compact(source_ref, i, 1, first)
+    for direction in (X, Y, T):
+        copies[direction].wait()
     solve(rho_ref, w_ref, applied_ref, masked_ref, link[0])
+    copies[Z].wait()
     half_w = scaled(load_spinor(w_ref), 0.5)
     store_faces(half_w, half_w, link[0], (t0_ref, t1_ref), (z0_ref, z1_ref))
     total = load_spinor(other_ref)
@@ -559,17 +575,22 @@
                 put(residual_ref, i, base_zero + zero[s][c][part], base_one + one[s][c][part])
 
 
-def call(kernel, shapes, operands, solver=False, moved=False, cost=3000000):
+def call(kernel, shapes, operands, solver=False, moved=False, fetch=False, cost=3000000):
     scratch = []
     if solver:
         scratch = [pltpu.VMEM((24,) + TILE, F32), pltpu.VMEM((54,) + TILE, F32)]
     if moved:
         scratch.append(pltpu.VMEM((144,) + TILE, F32))
+    if fetch:
+        operands = [pltpu.with_memory_space_constraint(v, pltpu.HBM) for v in operands]
+        scratch.append(pltpu.VMEM((24, 8, 256), F32))
+        scratch.append(pltpu.SemaphoreType.DMA((5,)))
     vmem = pl.BlockSpec(memory_space=pltpu.VMEM)
+    place = pl.BlockSpec(memory_space=pltpu.HBM) if fetch else vmem
     return pl.pallas_call(
         kernel,
         out_shape=[jax.ShapeDtypeStruct(shape, F32) for shape in shapes],
-        in_specs=[vmem] * len(operands),
+        in_specs=[place] * len(operands),
         out_specs=[vmem] * len(shapes),
         scratch_shapes=scratch,
         compiler_params=pltpu.CompilerParams(vmem_limit_bytes=12 << 20),
@@ -608,8 +629,12 @@
     source = source.reshape((24, 8, 256))
     spinor, half, quarter, rows = (24,) + TILE, (12,) + TILE, (6,) + TILE, (12, 128)
     faces = [rows] * 2 + [half] * 2
-    w0, rho0, other, *sent, packed = call(
-        kernel_one, [spinor] * 3 + faces + [(84,) + TILE], [links, source], solver=True
+    w0, rho0, other, *sent, packed, links = call(
+        kernel_one,
+        [spinor] * 3 + faces + [(84,) + TILE, (72, 8, 256)],
+        [links, source],
+        solver=True,
+        fetch=True,
     )
     moved = moved_to(packed, 1, 0)
     came = exchange_faces(*sent)

time: 59.9 us -> 59 us (0.985)
  local copies, waits for them, and re-layouts: 1.98 us -> 0 us
  Pallas kernels: 5.94 us -> 7.13 us
    unnamed x4 -> x0, local copies, waits for them, and re-layouts: 1.98 us -> none
    pallas_call x5, Pallas kernels: 5.94 us -> 7.13 us  [call(): pl.pallas_call(kernel, out_shape=[jax.ShapeDtypeStruct(shape, F32) for sh...]
where the time goes in v2:
time: 59 us; the launch traced here: 58.9 us
  starting transfers between devices  38.4 us (65%)
  waiting for transfers between devices  12.7 us (22%)
  Pallas kernels  7.13 us (12%)
  between operations  0.68 us (1%)
    ppermute x12, starting transfers between devices, exchanged(): return lax.ppermute(value, axis, pairs)  23 us
    ppermute x12, waiting for transfers between devices, exchanged(): return lax.ppermute(value, axis, pairs)  9.33 us
    ppermute x2, starting transfers between devices, moved_to(): return lax.ppermute(value, ('ta', 'gz'), pairs)  7.93 us
    ppermute x3, starting transfers between devices, moved_to(): lax.ppermute(value, 'ta', [(i, (i + time_steps) % times) for i in range(t...  7.47 us
    pallas_call x5, Pallas kernels, call(): pl.pallas_call(kernel, out_shape=[jax.ShapeDtypeStruct(shape, F32) for sh...  7.13 us
    ppermute x2, waiting for transfers between devices, moved_to(): return lax.ppermute(value, ('ta', 'gz'), pairs)  3.38 us
  transfers between devices with their start and end apart: 17, of which 7 were waited for; matrix products, arithmetic and copies ran while one was open for 0% of the time, Pallas kernels for 2%

profile of v2, /device:TPU:1, one launch (start us, length us, event | category | flops | bytes accessed | tf_op | source)
XLA Modules:
  0.0 58.9 jit_solution(11325218831416178324)
XLA Ops:
  0.6 2.4 %shard_map.41 = (f32[24,8,128]{2,1,0:T(8,128)S(1)}, f32[24,8,128]{2,1,0:T(8,128)S(1)}, f32[24,8,128]{2,1,0:T(8,128)S(1)}, f32[12,128]{1,0:T(8,128)S(1)}, f32[12,...) custom-call(f32[72,8,256]{2,1,0:T(8,128)} %bitcast.8, ...), custom_call_target="tpu_custom_call" | custom-call | flops 3000000 | bytes 1500000 | tf_op jit(solution)/shard_map/pallas_call | solution.py:590
  3.1 3.1 %collective-permute-start.4 = (f32[84,8,128]{2,1,0:T(8,128)S(1)}, f32[84,8,128]{2,1,0:T(8,128)S(1)}, u32[]{:S(2)}, u32[]{:S(2)}) collective-permute-start(f32[84,8,128]{2,1,0:T(8,128)S(1)} %get-tuple-element.45), channel_id=1, source_target_pairs={{0,4},{4,8},{8,12},{12,16},{16,20},{20,24},{24,28},{28,32},{32,36}... | collective-permute-start | bytes 1032200 | tf_op jit(solution)/shard_map/ppermute | solution.py:604
  6.2 3.0 %collective-permute-start.2 = (f32[12,8,128]{2,1,0:T(8,128)S(1)}, f32[12,8,128]{2,1,0:T(8,128)S(1)}, u32[]{:S(2)}, u32[]{:S(2)}) collective-permute-start(f32[12,8,128]{2,1,0:T(8,128)S(1)} %get-tuple-element.42), channel_id=1, source_target_pairs={{0,1},{1,0},{2,3},{3,2},{4,5},{5,4},{6,7},{7,6},{8,9},{9,8},{10,11... | collective-permute-start | bytes 147464 | tf_op jit(solution)/shard_map/ppermute | solution.py:616
  9.2 3.3 %collective-permute-start.3 = (f32[12,8,128]{2,1,0:T(8,128)S(1)}, f32[12,8,128]{2,1,0:T(8,128)S(1)}, u32[]{:S(2)}, u32[]{:S(2)}) collective-permute-start(f32[12,8,128]{2,1,0:T(8,128)S(1)} %get-tuple-element.43), channel_id=1, source_target_pairs={{0,3},{1,2},{2,1},{3,0},{4,7},{5,6},{6,5},{7,4},{8,11},{9,10},{10,... | collective-permute-start | bytes 147464 | tf_op jit(solution)/shard_map/ppermute | solution.py:616
  12.5 0.0 collective-permute-start
  12.5 2.1 %collective-permute-start.1 = (f32[12,128]{1,0:T(8,128)S(1)}, f32[12,128]{1,0:T(8,128)S(1)}, u32[]{:S(2)}, u32[]{:S(2)}) collective-permute-start(f32[12,128]{1,0:T(8,128)S(1)} %get-tuple-element.41), channel_id=1, source_target_pairs={{0,252},{4,8},{8,4},{12,16},{16,12},{20,24},{24,20},{28,32},{32,28... | collective-permute-start | bytes 18440 | tf_op jit(solution)/shard_map/ppermute | solution.py:616
  14.6 1.6 %collective-permute-done.1.t1_in = f32[12,128]{1,0:T(8,128)S(1)} collective-permute-done((f32[12,128]{1,0:T(8,128)S(1)}, f32[12,128]{1,0:T(8,128)S(1)}, u32[]{:S(2)}, u32[]{:S(2)}) %collective-permute-start.1) | collective-permute-done | bytes 6176 | tf_op jit(solution)/shard_map/ppermute | solution.py:616
  16.2 0.0 collective-permute-done.2.z0_in
  16.2 1.8 %collective-permute-done.3.z1_in = f32[12,8,128]{2,1,0:T(8,128)S(1)} collective-permute-done((f32[12,8,128]{2,1,0:T(8,128)S(1)}, f32[12,8,128]{2,1,0:T(8,128)S(1)}, u32[]{:S(2)}, u32[]{:S(2)}) %collective-permute-start.3) | collective-permute-done | bytes 49184 | tf_op jit(solution)/shard_map/ppermute | solution.py:616
  18.0 1.2 %shard_map.42 = (f32[24,8,128]{2,1,0:T(8,128)S(1)}, f32[24,8,128]{2,1,0:T(8,128)S(1)}, f32[24,8,128]{2,1,0:T(8,128)S(1)}, f32[24,8,128]{2,1,0:T(8,128)S(1)}, f32...) custom-call(f32[72,8,256]{2,1,0:T(8,128)S(1)} %get-tuple-element.36.links_ref, ...), custom_call_target="tpu_custom_call" | custom-call | flops 3000000 | bytes 1500000 | tf_op jit(solution)/shard_map/pallas_call | solution.py:590
  19.3 0.1 collective-permute-start.5
  19.4 0.8 %collective-permute-start.6 = (f32[6,8,128]{2,1,0:T(8,128)S(1)}, f32[6,8,128]{2,1,0:T(8,128)S(1)}, u32[]{:S(2)}, u32[]{:S(2)}) collective-permute-start(f32[6,8,128]{2,1,0:T(8,128)S(1)} %get-tuple-element.50), channel_id=1, source_target_pairs={{0,1},{1,0},{2,3},{3,2},{4,5},{5,4},{6,7},{7,6},{8,9},{9,8},{10,11... | collective-permute-start | bytes 73736 | tf_op jit(solution)/shard_map/ppermute | solution.py:616
  20.2 2.0 %collective-permute-start.7 = (f32[6,8,128]{2,1,0:T(8,128)S(1)}, f32[6,8,128]{2,1,0:T(8,128)S(1)}, u32[]{:S(2)}, u32[]{:S(2)}) collective-permute-start(f32[6,8,128]{2,1,0:T(8,128)S(1)} %get-tuple-element.51), channel_id=1, source_target_pairs={{0,3},{1,2},{2,1},{3,0},{4,7},{5,6},{6,5},{7,4},{8,11},{9,10},{10,... | collective-permute-start | bytes 73736 | tf_op jit(solution)/shard_map/ppermute | solution.py:616
  22.2 0.9 %collective-permute-done.6.z0_in = f32[6,8,128]{2,1,0:T(8,128)S(1)} collective-permute-done((f32[6,8,128]{2,1,0:T(8,128)S(1)}, f32[6,8,128]{2,1,0:T(8,128)S(1)}, u32[]{:S(2)}, u32[]{:S(2)}) %collective-permute-start.6) | collective-permute-done | bytes 24608 | tf_op jit(solution)/shard_map/ppermute | solution.py:616
  23.0 2.0 %collective-permute-done.7.z1_in = f32[6,8,128]{2,1,0:T(8,128)S(1)} collective-permute-done((f32[6,8,128]{2,1,0:T(8,128)S(1)}, f32[6,8,128]{2,1,0:T(8,128)S(1)}, u32[]{:S(2)}, u32[]{:S(2)}) %collective-permute-start.7) | collective-permute-done | bytes 24608 | tf_op jit(solution)/shard_map/ppermute | solution.py:616
  25.0 0.0 collective-permute-done.5.received
  25.0 0.0 collective-permute-done.4.moved_in
  25.0 1.3 %shard_map.43 = (f32[24,8,128]{2,1,0:T(8,128)S(1)}, f32[24,8,128]{2,1,0:T(8,128)S(1)}, f32[24,8,128]{2,1,0:T(8,128)S(1)}, f32[12,128]{1,0:T(8,128)S(1)}, f32[12,...) custom-call(f32[72,8,256]{2,1,0:T(8,128)S(1)} %get-tuple-element.36.links_ref, ...), custom_call_target="tpu_custom_call" | custom-call | flops 3000000 | bytes 1500000 | tf_op jit(solution)/shard_map/pallas_call | solution.py:590
  26.3 1.7 %collective-permute-start.10 = (f32[12,8,128]{2,1,0:T(8,128)S(1)}, f32[12,8,128]{2,1,0:T(8,128)S(1)}, u32[]{:S(2)}, u32[]{:S(2)}) collective-permute-start(f32[12,8,128]{2,1,0:T(8,128)S(1)} %get-tuple-element.57), channel_id=1, source_target_pairs={{0,1},{1,0},{2,3},{3,2},{4,5},{5,4},{6,7},{7,6},{8,9},{9,8},{10,11... | collective-permute-start | bytes 147464 | tf_op jit(solution)/shard_map/ppermute | solution.py:616
  28.0 2.1 %collective-permute-start.11 = (f32[12,8,128]{2,1,0:T(8,128)S(1)}, f32[12,8,128]{2,1,0:T(8,128)S(1)}, u32[]{:S(2)}, u32[]{:S(2)}) collective-permute-start(f32[12,8,128]{2,1,0:T(8,128)S(1)} %get-tuple-element.58), channel_id=1, source_target_pairs={{0,3},{1,2},{2,1},{3,0},{4,7},{5,6},{6,5},{7,4},{8,11},{9,10},{10,... | collective-permute-start | bytes 147464 | tf_op jit(solution)/shard_map/ppermute | solution.py:616
  30.1 6.5 %collective-permute-start.8 = (f32[12,128]{1,0:T(8,128)S(1)}, f32[12,128]{1,0:T(8,128)S(1)}, u32[]{:S(2)}, u32[]{:S(2)}) collective-permute-start(f32[12,128]{1,0:T(8,128)S(1)} %get-tuple-element.55), channel_id=1, source_target_pairs={{0,4},{4,0},{8,12},{12,8},{16,20},{20,16},{24,28},{28,24},{32,36},... | collective-permute-start | bytes 18440 | tf_op jit(solution)/shard_map/ppermute | solution.py:616
  36.6 0.0 collective-permute-start.9
  36.6 0.8 %collective-permute-done.8.t0_in = f32[12,128]{1,0:T(8,128)S(1)} collective-permute-done((f32[12,128]{1,0:T(8,128)S(1)}, f32[12,128]{1,0:T(8,128)S(1)}, u32[]{:S(2)}, u32[]{:S(2)}) %collective-permute-start.8) | collective-permute-done | bytes 6176 | tf_op jit(solution)/shard_map/ppermute | solution.py:616
  37.4 2.2 %collective-permute-done.9.t1_in = f32[12,128]{1,0:T(8,128)S(1)} collective-permute-done((f32[12,128]{1,0:T(8,128)S(1)}, f32[12,128]{1,0:T(8,128)S(1)}, u32[]{:S(2)}, u32[]{:S(2)}) %collective-permute-start.9) | collective-permute-done | bytes 6176 | tf_op jit(solution)/shard_map/ppermute | solution.py:616
  39.7 1.3 %shard_map.44 = (f32[24,8,128]{2,1,0:T(8,128)S(1)}, f32[24,8,128]{2,1,0:T(8,128)S(1)}, f32[24,8,128]{2,1,0:T(8,128)S(1)}, f32[48,8,128]{2,1,0:T(8,128)S(1)}, f32...) custom-call(f32[72,8,256]{2,1,0:T(8,128)S(1)} %get-tuple-element.36., ...), custom_call_target="tpu_custom_call" | custom-call | flops 3000000 | bytes 1500000 | tf_op jit(solution)/shard_map/pallas_call | solution.py:590
  41.0 4.3 %collective-permute-start.12 = (f32[48,8,128]{2,1,0:T(8,128)S(1)}, f32[48,8,128]{2,1,0:T(8,128)S(1)}, u32[]{:S(2)}, u32[]{:S(2)}) collective-permute-start(f32[48,8,128]{2,1,0:T(8,128)S(1)} %get-tuple-element.63), channel_id=1, source_target_pairs={{0,252},{4,0},{8,4},{12,8},{16,12},{20,16},{24,20},{28,24},{32,28}... | collective-permute-start | bytes 589832 | tf_op jit(solution)/shard_map/ppermute | solution.py:604
  45.3 0.4 collective-permute-start.13
  45.7 1.1 %collective-permute-start.14 = (f32[6,8,128]{2,1,0:T(8,128)S(1)}, f32[6,8,128]{2,1,0:T(8,128)S(1)}, u32[]{:S(2)}, u32[]{:S(2)}) collective-permute-start(f32[6,8,128]{2,1,0:T(8,128)S(1)} %get-tuple-element.65), channel_id=1, source_target_pairs={{0,3},{1,2},{2,1},{3,0},{4,7},{5,6},{6,5},{7,4},{8,11},{9,10},{10,... | collective-permute-start | bytes 73736 | tf_op jit(solution)/shard_map/ppermute | solution.py:616
  46.8 6.3 %collective-permute-start.15 = (f32[6,8,128]{2,1,0:T(8,128)S(1)}, f32[6,8,128]{2,1,0:T(8,128)S(1)}, u32[]{:S(2)}, u32[]{:S(2)}) collective-permute-start(f32[6,8,128]{2,1,0:T(8,128)S(1)} %get-tuple-element.66), channel_id=1, source_target_pairs={{0,253},{1,254},{2,255},{3,252},{4,1},{5,2},{6,3},{7,0},{8,5},{9,6... | collective-permute-start | bytes 73736 | tf_op jit(solution)/shard_map/ppermute | solution.py:610
  53.0 1.7 %collective-permute-start.16 = (f32[6,8,128]{2,1,0:T(8,128)S(1)}, f32[6,8,128]{2,1,0:T(8,128)S(1)}, u32[]{:S(2)}, u32[]{:S(2)}) collective-permute-start(f32[6,8,128]{2,1,0:T(8,128)S(1)} %get-tuple-element.67), channel_id=1, source_target_pairs={{0,255},{1,252},{2,253},{3,254},{4,3},{5,0},{6,1},{7,2},{8,7},{9,4... | collective-permute-start | bytes 73736 | tf_op jit(solution)/shard_map/ppermute | solution.py:610
  54.7 3.4 %collective-permute-done.16.zb_in = f32[6,8,128]{2,1,0:T(8,128)S(1)} collective-permute-done((f32[6,8,128]{2,1,0:T(8,128)S(1)}, f32[6,8,128]{2,1,0:T(8,128)S(1)}, u32[]{:S(2)}, u32[]{:S(2)}) %collective-permute-start.16) | collective-permute-done | bytes 24608 | tf_op jit(solution)/shard_map/ppermute | solution.py:610
  58.1 0.8 %shard_map.45 = (f32[24,8,256]{2,1,0:T(8,128)}, f32[24,8,256]{2,1,0:T(8,128)}) custom-call(f32[72,8,256]{2,1,0:T(8,128)S(1)} %get-tuple-element.36.links_ref, f32[24,8,128]{2,1,0:T(8,128)S(1)} %get-tuple-element.37.w0_ref, f32[24,8,128]{2,1,0:T(8,128)S(1)} %get-tuple-element.44.w1_ref, f32[24,8,128]{2,1,0:T(8,128)S(1)} %get-tuple-element.52.w_in.x0_ref, ...), custom_call_target="tpu_custom_call" | custom-call | flops 3000000 | bytes 1500000 | tf_op jit(solution)/shard_map/pallas_call | solution.py:590
  (7 shorter events, 0.0 us)
Async XLA Ops:
  3.1 21.9 %collective-permute-start.4 = (f32[84,8,128]{2,1,0:T(8,128)S(1)}, f32[84,8,128]{2,1,0:T(8,128)S(1)}, u32[]{:S(2)}, u32[]{:S(2)}) collective-permute-start(f32[84,8,128]{2,1,0:T(8,128)S(1)} %get-tuple-element.45), channel_id=1, source_target_pairs={{0,4},{4,8},{8,12},{12,16},{16,20},{20,24},{24,28},{28,32},{32,36}... | collective-permute-start | bytes 1032200 | tf_op jit(solution)/shard_map/ppermute | solution.py:604
  6.2 10.1 %collective-permute-start.2 = (f32[12,8,128]{2,1,0:T(8,128)S(1)}, f32[12,8,128]{2,1,0:T(8,128)S(1)}, u32[]{:S(2)}, u32[]{:S(2)}) collective-permute-start(f32[12,8,128]{2,1,0:T(8,128)S(1)} %get-tuple-element.42), channel_id=1, source_target_pairs={{0,1},{1,0},{2,3},{3,2},{4,5},{5,4},{6,7},{7,6},{8,9},{9,8},{10,11... | collective-permute-start | bytes 147464 | tf_op jit(solution)/shard_map/ppermute | solution.py:616
  9.2 8.9 %collective-permute-start.3 = (f32[12,8,128]{2,1,0:T(8,128)S(1)}, f32[12,8,128]{2,1,0:T(8,128)S(1)}, u32[]{:S(2)}, u32[]{:S(2)}) collective-permute-start(f32[12,8,128]{2,1,0:T(8,128)S(1)} %get-tuple-element.43), channel_id=1, source_target_pairs={{0,3},{1,2},{2,1},{3,0},{4,7},{5,6},{6,5},{7,4},{8,11},{9,10},{10,... | collective-permute-start | bytes 147464 | tf_op jit(solution)/shard_map/ppermute | solution.py:616
  12.5 2.1 %collective-permute-start = (f32[12,128]{1,0:T(8,128)S(1)}, f32[12,128]{1,0:T(8,128)S(1)}, u32[]{:S(2)}, u32[]{:S(2)}) collective-permute-start(f32[12,128]{1,0:T(8,128)S(1)} %get-tuple-element.40), channel_id=1, source_target_pairs={{0,4},{4,0},{8,12},{12,8},{16,20},{20,16},{24,28},{28,24},{32,36},... | collective-permute-start | bytes 18440 | tf_op jit(solution)/shard_map/ppermute | solution.py:616
  12.5 3.7 %collective-permute-start.1 = (f32[12,128]{1,0:T(8,128)S(1)}, f32[12,128]{1,0:T(8,128)S(1)}, u32[]{:S(2)}, u32[]{:S(2)}) collective-permute-start(f32[12,128]{1,0:T(8,128)S(1)} %get-tuple-element.41), channel_id=1, source_target_pairs={{0,252},{4,8},{8,4},{12,16},{16,12},{20,24},{24,20},{28,32},{32,28... | collective-permute-start | bytes 18440 | tf_op jit(solution)/shard_map/ppermute | solution.py:616
  19.3 5.7 %collective-permute-start.5 = (f32[24,8,128]{2,1,0:T(8,128)S(1)}, f32[24,8,128]{2,1,0:T(8,128)S(1)}, u32[]{:S(2)}, u32[]{:S(2)}) collective-permute-start(f32[24,8,128]{2,1,0:T(8,128)S(1)} %get-tuple-element.49), channel_id=1, source_target_pairs={{0,4},{4,8},{8,12},{12,16},{16,20},{20,24},{24,28},{28,32},{32,36}... | collective-permute-start | bytes 294920 | tf_op jit(solution)/shard_map/ppermute | solution.py:604
  19.4 3.7 %collective-permute-start.6 = (f32[6,8,128]{2,1,0:T(8,128)S(1)}, f32[6,8,128]{2,1,0:T(8,128)S(1)}, u32[]{:S(2)}, u32[]{:S(2)}) collective-permute-start(f32[6,8,128]{2,1,0:T(8,128)S(1)} %get-tuple-element.50), channel_id=1, source_target_pairs={{0,1},{1,0},{2,3},{3,2},{4,5},{5,4},{6,7},{7,6},{8,9},{9,8},{10,11... | collective-permute-start | bytes 73736 | tf_op jit(solution)/shard_map/ppermute | solution.py:616
  20.2 4.8 %collective-permute-start.7 = (f32[6,8,128]{2,1,0:T(8,128)S(1)}, f32[6,8,128]{2,1,0:T(8,128)S(1)}, u32[]{:S(2)}, u32[]{:S(2)}) collective-permute-start(f32[6,8,128]{2,1,0:T(8,128)S(1)} %get-tuple-element.51), channel_id=1, source_target_pairs={{0,3},{1,2},{2,1},{3,0},{4,7},{5,6},{6,5},{7,4},{8,11},{9,10},{10,... | collective-permute-start | bytes 73736 | tf_op jit(solution)/shard_map/ppermute | solution.py:616
  26.3 13.3 %collective-permute-start.10 = (f32[12,8,128]{2,1,0:T(8,128)S(1)}, f32[12,8,128]{2,1,0:T(8,128)S(1)}, u32[]{:S(2)}, u32[]{:S(2)}) collective-permute-start(f32[12,8,128]{2,1,0:T(8,128)S(1)} %get-tuple-element.57), channel_id=1, source_target_pairs={{0,1},{1,0},{2,3},{3,2},{4,5},{5,4},{6,7},{7,6},{8,9},{9,8},{10,11... | collective-permute-start | bytes 147464 | tf_op jit(solution)/shard_map/ppermute | solution.py:616
  28.0 11.6 %collective-permute-start.11 = (f32[12,8,128]{2,1,0:T(8,128)S(1)}, f32[12,8,128]{2,1,0:T(8,128)S(1)}, u32[]{:S(2)}, u32[]{:S(2)}) collective-permute-start(f32[12,8,128]{2,1,0:T(8,128)S(1)} %get-tuple-element.58), channel_id=1, source_target_pairs={{0,3},{1,2},{2,1},{3,0},{4,7},{5,6},{6,5},{7,4},{8,11},{9,10},{10,... | collective-permute-start | bytes 147464 | tf_op jit(solution)/shard_map/ppermute | solution.py:616
  30.1 7.3 %collective-permute-start.8 = (f32[12,128]{1,0:T(8,128)S(1)}, f32[12,128]{1,0:T(8,128)S(1)}, u32[]{:S(2)}, u32[]{:S(2)}) collective-permute-start(f32[12,128]{1,0:T(8,128)S(1)} %get-tuple-element.55), channel_id=1, source_target_pairs={{0,4},{4,0},{8,12},{12,8},{16,20},{20,16},{24,28},{28,24},{32,36},... | collective-permute-start | bytes 18440 | tf_op jit(solution)/shard_map/ppermute | solution.py:616
  36.6 3.1 %collective-permute-start.9 = (f32[12,128]{1,0:T(8,128)S(1)}, f32[12,128]{1,0:T(8,128)S(1)}, u32[]{:S(2)}, u32[]{:S(2)}) collective-permute-start(f32[12,128]{1,0:T(8,128)S(1)} %get-tuple-element.56), channel_id=1, source_target_pairs={{0,252},{4,8},{8,4},{12,16},{16,12},{20,24},{24,20},{28,32},{32,28... | collective-permute-start | bytes 18440 | tf_op jit(solution)/shard_map/ppermute | solution.py:616
  41.0 17.1 %collective-permute-start.12 = (f32[48,8,128]{2,1,0:T(8,128)S(1)}, f32[48,8,128]{2,1,0:T(8,128)S(1)}, u32[]{:S(2)}, u32[]{:S(2)}) collective-permute-start(f32[48,8,128]{2,1,0:T(8,128)S(1)} %get-tuple-element.63), channel_id=1, source_target_pairs={{0,252},{4,0},{8,4},{12,8},{16,12},{20,16},{24,20},{28,24},{32,28}... | collective-permute-start | bytes 589832 | tf_op jit(solution)/shard_map/ppermute | solution.py:604
  45.3 9.4 %collective-permute-start.13 = (f32[6,8,128]{2,1,0:T(8,128)S(1)}, f32[6,8,128]{2,1,0:T(8,128)S(1)}, u32[]{:S(2)}, u32[]{:S(2)}) collective-permute-start(f32[6,8,128]{2,1,0:T(8,128)S(1)} %get-tuple-element.64), channel_id=1, source_target_pairs={{0,1},{1,0},{2,3},{3,2},{4,5},{5,4},{6,7},{7,6},{8,9},{9,8},{10,11... | collective-permute-start | bytes 73736 | tf_op jit(solution)/shard_map/ppermute | solution.py:616
  45.7 9.0 %collective-permute-start.14 = (f32[6,8,128]{2,1,0:T(8,128)S(1)}, f32[6,8,128]{2,1,0:T(8,128)S(1)}, u32[]{:S(2)}, u32[]{:S(2)}) collective-permute-start(f32[6,8,128]{2,1,0:T(8,128)S(1)} %get-tuple-element.65), channel_id=1, source_target_pairs={{0,3},{1,2},{2,1},{3,0},{4,7},{5,6},{6,5},{7,4},{8,11},{9,10},{10,... | collective-permute-start | bytes 73736 | tf_op jit(solution)/shard_map/ppermute | solution.py:616
  46.8 7.9 %collective-permute-start.15 = (f32[6,8,128]{2,1,0:T(8,128)S(1)}, f32[6,8,128]{2,1,0:T(8,128)S(1)}, u32[]{:S(2)}, u32[]{:S(2)}) collective-permute-start(f32[6,8,128]{2,1,0:T(8,128)S(1)} %get-tuple-element.66), channel_id=1, source_target_pairs={{0,253},{1,254},{2,255},{3,252},{4,1},{5,2},{6,3},{7,0},{8,5},{9,6... | collective-permute-start | bytes 73736 | tf_op jit(solution)/shard_map/ppermute | solution.py:610
  53.0 5.0 %collective-permute-start.16 = (f32[6,8,128]{2,1,0:T(8,128)S(1)}, f32[6,8,128]{2,1,0:T(8,128)S(1)}, u32[]{:S(2)}, u32[]{:S(2)}) collective-permute-start(f32[6,8,128]{2,1,0:T(8,128)S(1)} %get-tuple-element.67), channel_id=1, source_target_pairs={{0,255},{1,252},{2,253},{3,254},{4,3},{5,0},{6,1},{7,2},{8,7},{9,4... | collective-permute-start | bytes 73736 | tf_op jit(solution)/shard_map/ppermute | solution.py:610

commit v3 on v2

--- a/solution.py
+++ b/solution.py
@@ -461,8 +461,8 @@
 
 
 def kernel_three(links_ref, moved_in, rest_in, rho_in, tb_in, received, z0_in, z1_in,
-                 w_ref, rho_ref, other_ref, t0_ref, t1_ref, z0_ref, z1_ref,
-                 applied_ref, masked_ref, moved_ref):
+                 w_ref, rho_ref, other_ref, t0_ref, t1_ref, z0_ref, z1_ref, moved_ref,
+                 applied_ref, masked_ref):
     fill_moved_links(moved_ref, links_ref, moved_in)
     link = moved_links(moved_ref)
     time = time_ids()
@@ -499,10 +499,9 @@
     store_spinor(other_ref, total)
 
 
-def kernel_four(links_ref, moved_in, w_in, rho_in, other_in, t0_in, t1_in, z0_in, z1_in,
+def kernel_four(moved_ref, w_in, rho_in, other_in, t0_in, t1_in, z0_in, z1_in,
                 w_ref, rest_ref, rho_ref, send_ref, ta_ref, z0_ref, z1_ref, za_ref, zb_ref,
-                applied_ref, masked_ref, moved_ref):
-    fill_moved_links(moved_ref, links_ref, moved_in)
+                applied_ref, masked_ref):
     link = moved_links(moved_ref)
     total = load_spinor(other_in)
     add_faces(total, link[1], (t0_in, t1_in), (z0_in, z1_in))
@@ -575,12 +574,10 @@
                 put(residual_ref, i, base_zero + zero[s][c][part], base_one + one[s][c][part])
 
 
-def call(kernel, shapes, operands, solver=False, moved=False, fetch=False, cost=3000000):
+def call(kernel, shapes, operands, solver=False, fetch=False, cost=3000000):
     scratch = []
     if solver:
         scratch = [pltpu.VMEM((24,) + TILE, F32), pltpu.VMEM((54,) + TILE, F32)]
-    if moved:
-        scratch.append(pltpu.VMEM((144,) + TILE, F32))
     if fetch:
         operands = [pltpu.with_memory_space_constraint(v, pltpu.HBM) for v in operands]
         scratch.append(pltpu.VMEM((24, 8, 256), F32))
@@ -647,20 +644,18 @@
     z0 = exchanged(z0, "gz", 0)
     z1 = exchanged(z1, "gz", 1)
     send = moved_to(send, 1, 0)
-    x0, rho0, other, *sent = call(
+    x0, rho0, other, *sent, moved = call(
         kernel_three,
-        [spinor] * 3 + faces,
+        [spinor] * 3 + faces + [(144,) + TILE],
         [links, moved, rest, rho1, tb, send, z0, z1],
         solver=True,
-        moved=True,
     )
     came = exchange_faces(*sent)
     x1, rest, rho1, send, ta, z0, z1, za, zb = call(
         kernel_four,
         [spinor] * 3 + [(48,) + TILE, rows] + [quarter] * 4,
-        [links, moved, x0, rho0, other] + came,
+        [moved, x0, rho0, other] + came,
         solver=True,
-        moved=True,
     )
     z0 = exchanged(z0, "gz", 0)
     z1 = exchanged(z1, "gz", 1)

time: 59 us -> 59 us (level)
  no operation moved by 1% of the time
where the time goes in v3:
time: 59 us; the launch traced here: 58.9 us
  starting transfers between devices  38.4 us (65%)
  waiting for transfers between devices  12.7 us (22%)
  Pallas kernels  7.09 us (12%)
  between operations  0.68 us (1%)
    ppermute x12, starting transfers between devices, exchanged(): return lax.ppermute(value, axis, pairs)  23 us
    ppermute x12, waiting for transfers between devices, exchanged(): return lax.ppermute(value, axis, pairs)  9.33 us
    ppermute x2, starting transfers between devices, moved_to(): return lax.ppermute(value, ('ta', 'gz'), pairs)  7.93 us
    ppermute x3, starting transfers between devices, moved_to(): lax.ppermute(value, 'ta', [(i, (i + time_steps) % times) for i in range(t...  7.47 us
    pallas_call x5, Pallas kernels, call(): pl.pallas_call(kernel, out_shape=[jax.ShapeDtypeStruct(shape, F32) for sh...  7.09 us
    ppermute x2, waiting for transfers between devices, moved_to(): return lax.ppermute(value, ('ta', 'gz'), pairs)  3.38 us
  transfers between devices with their start and end apart: 17, of which 7 were waited for; matrix products, arithmetic and copies ran while one was open for 0% of the time, Pallas kernels for 2%

profile of v3, /device:TPU:1, one launch (start us, length us, event | category | flops | bytes accessed | tf_op | source)
XLA Modules:
  0.0 58.9 jit_solution(17088172740496420838)
XLA Ops:
  0.6 2.4 %shard_map.41 = (f32[24,8,128]{2,1,0:T(8,128)S(1)}, f32[24,8,128]{2,1,0:T(8,128)S(1)}, f32[24,8,128]{2,1,0:T(8,128)S(1)}, f32[12,128]{1,0:T(8,128)S(1)}, f32[12,...) custom-call(f32[72,8,256]{2,1,0:T(8,128)} %bitcast.8, ...), custom_call_target="tpu_custom_call" | custom-call | flops 3000000 | bytes 1500000 | tf_op jit(solution)/shard_map/pallas_call | solution.py:587
  3.1 3.1 %collective-permute-start.4 = (f32[84,8,128]{2,1,0:T(8,128)S(1)}, f32[84,8,128]{2,1,0:T(8,128)S(1)}, u32[]{:S(2)}, u32[]{:S(2)}) collective-permute-start(f32[84,8,128]{2,1,0:T(8,128)S(1)} %get-tuple-element.46), channel_id=1, source_target_pairs={{0,4},{4,8},{8,12},{12,16},{16,20},{20,24},{24,28},{28,32},{32,36}... | collective-permute-start | bytes 1032200 | tf_op jit(solution)/shard_map/ppermute | solution.py:601
  6.2 3.0 %collective-permute-start.2 = (f32[12,8,128]{2,1,0:T(8,128)S(1)}, f32[12,8,128]{2,1,0:T(8,128)S(1)}, u32[]{:S(2)}, u32[]{:S(2)}) collective-permute-start(f32[12,8,128]{2,1,0:T(8,128)S(1)} %get-tuple-element.43), channel_id=1, source_target_pairs={{0,1},{1,0},{2,3},{3,2},{4,5},{5,4},{6,7},{7,6},{8,9},{9,8},{10,11... | collective-permute-start | bytes 147464 | tf_op jit(solution)/shard_map/ppermute | solution.py:613
  9.2 3.3 %collective-permute-start.3 = (f32[12,8,128]{2,1,0:T(8,128)S(1)}, f32[12,8,128]{2,1,0:T(8,128)S(1)}, u32[]{:S(2)}, u32[]{:S(2)}) collective-permute-start(f32[12,8,128]{2,1,0:T(8,128)S(1)} %get-tuple-element.44), channel_id=1, source_target_pairs={{0,3},{1,2},{2,1},{3,0},{4,7},{5,6},{6,5},{7,4},{8,11},{9,10},{10,... | collective-permute-start | bytes 147464 | tf_op jit(solution)/shard_map/ppermute | solution.py:613
  12.5 0.0 collective-permute-start
  12.5 2.1 %collective-permute-start.1 = (f32[12,128]{1,0:T(8,128)S(1)}, f32[12,128]{1,0:T(8,128)S(1)}, u32[]{:S(2)}, u32[]{:S(2)}) collective-permute-start(f32[12,128]{1,0:T(8,128)S(1)} %get-tuple-element.42), channel_id=1, source_target_pairs={{0,252},{4,8},{8,4},{12,16},{16,12},{20,24},{24,20},{28,32},{32,28... | collective-permute-start | bytes 18440 | tf_op jit(solution)/shard_map/ppermute | solution.py:613
  14.6 1.6 %collective-permute-done.1.t1_in = f32[12,128]{1,0:T(8,128)S(1)} collective-permute-done((f32[12,128]{1,0:T(8,128)S(1)}, f32[12,128]{1,0:T(8,128)S(1)}, u32[]{:S(2)}, u32[]{:S(2)}) %collective-permute-start.1) | collective-permute-done | bytes 6176 | tf_op jit(solution)/shard_map/ppermute | solution.py:613
  16.2 0.0 collective-permute-done.2.z0_in
  16.2 1.8 %collective-permute-done.3.z1_in = f32[12,8,128]{2,1,0:T(8,128)S(1)} collective-permute-done((f32[12,8,128]{2,1,0:T(8,128)S(1)}, f32[12,8,128]{2,1,0:T(8,128)S(1)}, u32[]{:S(2)}, u32[]{:S(2)}) %collective-permute-start.3) | collective-permute-done | bytes 49184 | tf_op jit(solution)/shard_map/ppermute | solution.py:613
  18.0 1.2 %shard_map.42 = (f32[24,8,128]{2,1,0:T(8,128)S(1)}, f32[24,8,128]{2,1,0:T(8,128)S(1)}, f32[24,8,128]{2,1,0:T(8,128)S(1)}, f32[24,8,128]{2,1,0:T(8,128)S(1)}, f32...) custom-call(f32[72,8,256]{2,1,0:T(8,128)S(1)} %get-tuple-element.37.links_ref, ...), custom_call_target="tpu_custom_call" | custom-call | flops 3000000 | bytes 1500000 | tf_op jit(solution)/shard_map/pallas_call | solution.py:587
  19.3 0.1 collective-permute-start.5
  19.4 0.8 %collective-permute-start.6 = (f32[6,8,128]{2,1,0:T(8,128)S(1)}, f32[6,8,128]{2,1,0:T(8,128)S(1)}, u32[]{:S(2)}, u32[]{:S(2)}) collective-permute-start(f32[6,8,128]{2,1,0:T(8,128)S(1)} %get-tuple-element.51), channel_id=1, source_target_pairs={{0,1},{1,0},{2,3},{3,2},{4,5},{5,4},{6,7},{7,6},{8,9},{9,8},{10,11... | collective-permute-start | bytes 73736 | tf_op jit(solution)/shard_map/ppermute | solution.py:613
  20.2 2.0 %collective-permute-start.7 = (f32[6,8,128]{2,1,0:T(8,128)S(1)}, f32[6,8,128]{2,1,0:T(8,128)S(1)}, u32[]{:S(2)}, u32[]{:S(2)}) collective-permute-start(f32[6,8,128]{2,1,0:T(8,128)S(1)} %get-tuple-element.52), channel_id=1, source_target_pairs={{0,3},{1,2},{2,1},{3,0},{4,7},{5,6},{6,5},{7,4},{8,11},{9,10},{10,... | collective-permute-start | bytes 73736 | tf_op jit(solution)/shard_map/ppermute | solution.py:613
  22.2 0.9 %collective-permute-done.6.z0_in = f32[6,8,128]{2,1,0:T(8,128)S(1)} collective-permute-done((f32[6,8,128]{2,1,0:T(8,128)S(1)}, f32[6,8,128]{2,1,0:T(8,128)S(1)}, u32[]{:S(2)}, u32[]{:S(2)}) %collective-permute-start.6) | collective-permute-done | bytes 24608 | tf_op jit(solution)/shard_map/ppermute | solution.py:613
  23.0 2.0 %collective-permute-done.7.z1_in = f32[6,8,128]{2,1,0:T(8,128)S(1)} collective-permute-done((f32[6,8,128]{2,1,0:T(8,128)S(1)}, f32[6,8,128]{2,1,0:T(8,128)S(1)}, u32[]{:S(2)}, u32[]{:S(2)}) %collective-permute-start.7) | collective-permute-done | bytes 24608 | tf_op jit(solution)/shard_map/ppermute | solution.py:613
  25.0 1.3 %shard_map.43 = (f32[24,8,128]{2,1,0:T(8,128)S(1)}, f32[24,8,128]{2,1,0:T(8,128)S(1)}, f32[24,8,128]{2,1,0:T(8,128)S(1)}, f32[12,128]{1,0:T(8,128)S(1)}, f32[12,...) custom-call(f32[72,8,256]{2,1,0:T(8,128)S(1)} %get-tuple-element.37.links_re, ...), custom_call_target="tpu_custom_call" | custom-call | flops 3000000 | bytes 1500000 | tf_op jit(solution)/shard_map/pallas_call | solution.py:587
  26.3 1.7 %collective-permute-start.10 = (f32[12,8,128]{2,1,0:T(8,128)S(1)}, f32[12,8,128]{2,1,0:T(8,128)S(1)}, u32[]{:S(2)}, u32[]{:S(2)}) collective-permute-start(f32[12,8,128]{2,1,0:T(8,128)S(1)} %get-tuple-element.59), channel_id=1, source_target_pairs={{0,1},{1,0},{2,3},{3,2},{4,5},{5,4},{6,7},{7,6},{8,9},{9,8},{10,11... | collective-permute-start | bytes 147464 | tf_op jit(solution)/shard_map/ppermute | solution.py:613
  28.0 2.1 %collective-permute-start.11 = (f32[12,8,128]{2,1,0:T(8,128)S(1)}, f32[12,8,128]{2,1,0:T(8,128)S(1)}, u32[]{:S(2)}, u32[]{:S(2)}) collective-permute-start(f32[12,8,128]{2,1,0:T(8,128)S(1)} %get-tuple-element.60), channel_id=1, source_target_pairs={{0,3},{1,2},{2,1},{3,0},{4,7},{5,6},{6,5},{7,4},{8,11},{9,10},{10,... | collective-permute-start | bytes 147464 | tf_op jit(solution)/shard_map/ppermute | solution.py:613
  30.1 6.5 %collective-permute-start.8 = (f32[12,128]{1,0:T(8,128)S(1)}, f32[12,128]{1,0:T(8,128)S(1)}, u32[]{:S(2)}, u32[]{:S(2)}) collective-permute-start(f32[12,128]{1,0:T(8,128)S(1)} %get-tuple-element.57), channel_id=1, source_target_pairs={{0,4},{4,0},{8,12},{12,8},{16,20},{20,16},{24,28},{28,24},{32,36},... | collective-permute-start | bytes 18440 | tf_op jit(solution)/shard_map/ppermute | solution.py:613
  36.6 0.0 collective-permute-start.9
  36.6 0.8 %collective-permute-done.8.t0_in = f32[12,128]{1,0:T(8,128)S(1)} collective-permute-done((f32[12,128]{1,0:T(8,128)S(1)}, f32[12,128]{1,0:T(8,128)S(1)}, u32[]{:S(2)}, u32[]{:S(2)}) %collective-permute-start.8) | collective-permute-done | bytes 6176 | tf_op jit(solution)/shard_map/ppermute | solution.py:613
  37.4 2.2 %collective-permute-done.9.t1_in = f32[12,128]{1,0:T(8,128)S(1)} collective-permute-done((f32[12,128]{1,0:T(8,128)S(1)}, f32[12,128]{1,0:T(8,128)S(1)}, u32[]{:S(2)}, u32[]{:S(2)}) %collective-permute-start.9) | collective-permute-done | bytes 6176 | tf_op jit(solution)/shard_map/ppermute | solution.py:613
  39.7 0.0 collective-permute-done.10.z0_in
  39.7 0.0 collective-permute-done.11.z1_in
  39.7 1.3 %shard_map.44 = (f32[24,8,128]{2,1,0:T(8,128)S(1)}, f32[24,8,128]{2,1,0:T(8,128)S(1)}, f32[24,8,128]{2,1,0:T(8,128)S(1)}, f32[48,8,128]{2,1,0:T(8,128)S(1)}, f32...) custom-call(f32[144,8,128]{2,1,0:T(8,128)S(1)} %get-tuple-element.54, ...), custom_call_target="tpu_custom_call" | custom-call | flops 3000000 | bytes 1500000 | tf_op jit(solution)/shard_map/pallas_call | solution.py:587
  40.9 4.3 %collective-permute-start.12 = (f32[48,8,128]{2,1,0:T(8,128)S(1)}, f32[48,8,128]{2,1,0:T(8,128)S(1)}, u32[]{:S(2)}, u32[]{:S(2)}) collective-permute-start(f32[48,8,128]{2,1,0:T(8,128)S(1)} %get-tuple-element.65), channel_id=1, source_target_pairs={{0,252},{4,0},{8,4},{12,8},{16,12},{20,16},{24,20},{28,24},{32,28}... | collective-permute-start | bytes 589832 | tf_op jit(solution)/shard_map/ppermute | solution.py:601
  45.2 0.4 collective-permute-start.13
  45.7 1.1 %collective-permute-start.14 = (f32[6,8,128]{2,1,0:T(8,128)S(1)}, f32[6,8,128]{2,1,0:T(8,128)S(1)}, u32[]{:S(2)}, u32[]{:S(2)}) collective-permute-start(f32[6,8,128]{2,1,0:T(8,128)S(1)} %get-tuple-element.67), channel_id=1, source_target_pairs={{0,3},{1,2},{2,1},{3,0},{4,7},{5,6},{6,5},{7,4},{8,11},{9,10},{10,... | collective-permute-start | bytes 73736 | tf_op jit(solution)/shard_map/ppermute | solution.py:613
  46.7 6.3 %collective-permute-start.15 = (f32[6,8,128]{2,1,0:T(8,128)S(1)}, f32[6,8,128]{2,1,0:T(8,128)S(1)}, u32[]{:S(2)}, u32[]{:S(2)}) collective-permute-start(f32[6,8,128]{2,1,0:T(8,128)S(1)} %get-tuple-element.68), channel_id=1, source_target_pairs={{0,253},{1,254},{2,255},{3,252},{4,1},{5,2},{6,3},{7,0},{8,5},{9,6... | collective-permute-start | bytes 73736 | tf_op jit(solution)/shard_map/ppermute | solution.py:607
  53.0 1.7 %collective-permute-start.16 = (f32[6,8,128]{2,1,0:T(8,128)S(1)}, f32[6,8,128]{2,1,0:T(8,128)S(1)}, u32[]{:S(2)}, u32[]{:S(2)}) collective-permute-start(f32[6,8,128]{2,1,0:T(8,128)S(1)} %get-tuple-element.69), channel_id=1, source_target_pairs={{0,255},{1,252},{2,253},{3,254},{4,3},{5,0},{6,1},{7,2},{8,7},{9,4... | collective-permute-start | bytes 73736 | tf_op jit(solution)/shard_map/ppermute | solution.py:607
  54.7 3.4 %collective-permute-done.16.zb_in = f32[6,8,128]{2,1,0:T(8,128)S(1)} collective-permute-done((f32[6,8,128]{2,1,0:T(8,128)S(1)}, f32[6,8,128]{2,1,0:T(8,128)S(1)}, u32[]{:S(2)}, u32[]{:S(2)}) %collective-permute-start.16) | collective-permute-done | bytes 24608 | tf_op jit(solution)/shard_map/ppermute | solution.py:607
  58.1 0.8 %shard_map.45 = (f32[24,8,256]{2,1,0:T(8,128)}, f32[24,8,256]{2,1,0:T(8,128)}) custom-call(f32[72,8,256]{2,1,0:T(8,128)S(1)} %get-tuple-element.37.links_ref, f32[24,8,128]{2,1,0:T(8,128)S(1)} %get-tuple-element.38.w0_ref, f32[24,8,128]{2,1,0:T(8,128)S(1)} %get-tuple-element.45.w1_ref, f32[24,8,128]{2,1,0:T(8,128)S(1)} %get-tuple-element.53.w_in.x0_ref, ...), custom_call_target="tpu_custom_call" | custom-call | flops 3000000 | bytes 1500000 | tf_op jit(solution)/shard_map/pallas_call | solution.py:587
  (7 shorter events, 0.0 us)
Async XLA Ops:
  3.1 21.9 %collective-permute-start.4 = (f32[84,8,128]{2,1,0:T(8,128)S(1)}, f32[84,8,128]{2,1,0:T(8,128)S(1)}, u32[]{:S(2)}, u32[]{:S(2)}) collective-permute-start(f32[84,8,128]{2,1,0:T(8,128)S(1)} %get-tuple-element.46), channel_id=1, source_target_pairs={{0,4},{4,8},{8,12},{12,16},{16,20},{20,24},{24,28},{28,32},{32,36}... | collective-permute-start | bytes 1032200 | tf_op jit(solution)/shard_map/ppermute | solution.py:601
  6.2 10.1 %collective-permute-start.2 = (f32[12,8,128]{2,1,0:T(8,128)S(1)}, f32[12,8,128]{2,1,0:T(8,128)S(1)}, u32[]{:S(2)}, u32[]{:S(2)}) collective-permute-start(f32[12,8,128]{2,1,0:T(8,128)S(1)} %get-tuple-element.43), channel_id=1, source_target_pairs={{0,1},{1,0},{2,3},{3,2},{4,5},{5,4},{6,7},{7,6},{8,9},{9,8},{10,11... | collective-permute-start | bytes 147464 | tf_op jit(solution)/shard_map/ppermute | solution.py:613
  9.2 8.9 %collective-permute-start.3 = (f32[12,8,128]{2,1,0:T(8,128)S(1)}, f32[12,8,128]{2,1,0:T(8,128)S(1)}, u32[]{:S(2)}, u32[]{:S(2)}) collective-permute-start(f32[12,8,128]{2,1,0:T(8,128)S(1)} %get-tuple-element.44), channel_id=1, source_target_pairs={{0,3},{1,2},{2,1},{3,0},{4,7},{5,6},{6,5},{7,4},{8,11},{9,10},{10,... | collective-permute-start | bytes 147464 | tf_op jit(solution)/shard_map/ppermute | solution.py:613
  12.5 2.1 %collective-permute-start = (f32[12,128]{1,0:T(8,128)S(1)}, f32[12,128]{1,0:T(8,128)S(1)}, u32[]{:S(2)}, u32[]{:S(2)}) collective-permute-start(f32[12,128]{1,0:T(8,128)S(1)} %get-tuple-element.41), channel_id=1, source_target_pairs={{0,4},{4,0},{8,12},{12,8},{16,20},{20,16},{24,28},{28,24},{32,36},... | collective-permute-start | bytes 18440 | tf_op jit(solution)/shard_map/ppermute | solution.py:613
  12.5 3.7 %collective-permute-start.1 = (f32[12,128]{1,0:T(8,128)S(1)}, f32[12,128]{1,0:T(8,128)S(1)}, u32[]{:S(2)}, u32[]{:S(2)}) collective-permute-start(f32[12,128]{1,0:T(8,128)S(1)} %get-tuple-element.42), channel_id=1, source_target_pairs={{0,252},{4,8},{8,4},{12,16},{16,12},{20,24},{24,20},{28,32},{32,28... | collective-permute-start | bytes 18440 | tf_op jit(solution)/shard_map/ppermute | solution.py:613
  19.3 5.7 %collective-permute-start.5 = (f32[24,8,128]{2,1,0:T(8,128)S(1)}, f32[24,8,128]{2,1,0:T(8,128)S(1)}, u32[]{:S(2)}, u32[]{:S(2)}) collective-permute-start(f32[24,8,128]{2,1,0:T(8,128)S(1)} %get-tuple-element.50), channel_id=1, source_target_pairs={{0,4},{4,8},{8,12},{12,16},{16,20},{20,24},{24,28},{28,32},{32,36}... | collective-permute-start | bytes 294920 | tf_op jit(solution)/shard_map/ppermute | solution.py:601
  19.4 3.7 %collective-permute-start.6 = (f32[6,8,128]{2,1,0:T(8,128)S(1)}, f32[6,8,128]{2,1,0:T(8,128)S(1)}, u32[]{:S(2)}, u32[]{:S(2)}) collective-permute-start(f32[6,8,128]{2,1,0:T(8,128)S(1)} %get-tuple-element.51), channel_id=1, source_target_pairs={{0,1},{1,0},{2,3},{3,2},{4,5},{5,4},{6,7},{7,6},{8,9},{9,8},{10,11... | collective-permute-start | bytes 73736 | tf_op jit(solution)/shard_map/ppermute | solution.py:613
  20.2 4.8 %collective-permute-start.7 = (f32[6,8,128]{2,1,0:T(8,128)S(1)}, f32[6,8,128]{2,1,0:T(8,128)S(1)}, u32[]{:S(2)}, u32[]{:S(2)}) collective-permute-start(f32[6,8,128]{2,1,0:T(8,128)S(1)} %get-tuple-element.52), channel_id=1, source_target_pairs={{0,3},{1,2},{2,1},{3,0},{4,7},{5,6},{6,5},{7,4},{8,11},{9,10},{10,... | collective-permute-start | bytes 73736 | tf_op jit(solution)/shard_map/ppermute | solution.py:613
  26.3 13.3 %collective-permute-start.10 = (f32[12,8,128]{2,1,0:T(8,128)S(1)}, f32[12,8,128]{2,1,0:T(8,128)S(1)}, u32[]{:S(2)}, u32[]{:S(2)}) collective-permute-start(f32[12,8,128]{2,1,0:T(8,128)S(1)} %get-tuple-element.59), channel_id=1, source_target_pairs={{0,1},{1,0},{2,3},{3,2},{4,5},{5,4},{6,7},{7,6},{8,9},{9,8},{10,11... | collective-permute-start | bytes 147464 | tf_op jit(solution)/shard_map/ppermute | solution.py:613
  28.0 11.6 %collective-permute-start.11 = (f32[12,8,128]{2,1,0:T(8,128)S(1)}, f32[12,8,128]{2,1,0:T(8,128)S(1)}, u32[]{:S(2)}, u32[]{:S(2)}) collective-permute-start(f32[12,8,128]{2,1,0:T(8,128)S(1)} %get-tuple-element.60), channel_id=1, source_target_pairs={{0,3},{1,2},{2,1},{3,0},{4,7},{5,6},{6,5},{7,4},{8,11},{9,10},{10,... | collective-permute-start | bytes 147464 | tf_op jit(solution)/shard_map/ppermute | solution.py:613
  30.1 7.3 %collective-permute-start.8 = (f32[12,128]{1,0:T(8,128)S(1)}, f32[12,128]{1,0:T(8,128)S(1)}, u32[]{:S(2)}, u32[]{:S(2)}) collective-permute-start(f32[12,128]{1,0:T(8,128)S(1)} %get-tuple-element.57), channel_id=1, source_target_pairs={{0,4},{4,0},{8,12},{12,8},{16,20},{20,16},{24,28},{28,24},{32,36},... | collective-permute-start | bytes 18440 | tf_op jit(solution)/shard_map/ppermute | solution.py:613
  36.6 3.1 %collective-permute-start.9 = (f32[12,128]{1,0:T(8,128)S(1)}, f32[12,128]{1,0:T(8,128)S(1)}, u32[]{:S(2)}, u32[]{:S(2)}) collective-permute-start(f32[12,128]{1,0:T(8,128)S(1)} %get-tuple-element.58), channel_id=1, source_target_pairs={{0,252},{4,8},{8,4},{12,16},{16,12},{20,24},{24,20},{28,32},{32,28... | collective-permute-start | bytes 18440 | tf_op jit(solution)/shard_map/ppermute | solution.py:613
  40.9 17.1 %collective-permute-start.12 = (f32[48,8,128]{2,1,0:T(8,128)S(1)}, f32[48,8,128]{2,1,0:T(8,128)S(1)}, u32[]{:S(2)}, u32[]{:S(2)}) collective-permute-start(f32[48,8,128]{2,1,0:T(8,128)S(1)} %get-tuple-element.65), channel_id=1, source_target_pairs={{0,252},{4,0},{8,4},{12,8},{16,12},{20,16},{24,20},{28,24},{32,28}... | collective-permute-start | bytes 589832 | tf_op jit(solution)/shard_map/ppermute | solution.py:601
  45.2 9.4 %collective-permute-start.13 = (f32[6,8,128]{2,1,0:T(8,128)S(1)}, f32[6,8,128]{2,1,0:T(8,128)S(1)}, u32[]{:S(2)}, u32[]{:S(2)}) collective-permute-start(f32[6,8,128]{2,1,0:T(8,128)S(1)} %get-tuple-element.66), channel_id=1, source_target_pairs={{0,1},{1,0},{2,3},{3,2},{4,5},{5,4},{6,7},{7,6},{8,9},{9,8},{10,11... | collective-permute-start | bytes 73736 | tf_op jit(solution)/shard_map/ppermute | solution.py:613
  45.7 9.0 %collective-permute-start.14 = (f32[6,8,128]{2,1,0:T(8,128)S(1)}, f32[6,8,128]{2,1,0:T(8,128)S(1)}, u32[]{:S(2)}, u32[]{:S(2)}) collective-permute-start(f32[6,8,128]{2,1,0:T(8,128)S(1)} %get-tuple-element.67), channel_id=1, source_target_pairs={{0,3},{1,2},{2,1},{3,0},{4,7},{5,6},{6,5},{7,4},{8,11},{9,10},{10,... | collective-permute-start | bytes 73736 | tf_op jit(solution)/shard_map/ppermute | solution.py:613
  46.7 7.9 %collective-permute-start.15 = (f32[6,8,128]{2,1,0:T(8,128)S(1)}, f32[6,8,128]{2,1,0:T(8,128)S(1)}, u32[]{:S(2)}, u32[]{:S(2)}) collective-permute-start(f32[6,8,128]{2,1,0:T(8,128)S(1)} %get-tuple-element.68), channel_id=1, source_target_pairs={{0,253},{1,254},{2,255},{3,252},{4,1},{5,2},{6,3},{7,0},{8,5},{9,6... | collective-permute-start | bytes 73736 | tf_op jit(solution)/shard_map/ppermute | solution.py:607
  53.0 5.0 %collective-permute-start.16 = (f32[6,8,128]{2,1,0:T(8,128)S(1)}, f32[6,8,128]{2,1,0:T(8,128)S(1)}, u32[]{:S(2)}, u32[]{:S(2)}) collective-permute-start(f32[6,8,128]{2,1,0:T(8,128)S(1)} %get-tuple-element.69), channel_id=1, source_target_pairs={{0,255},{1,252},{2,253},{3,254},{4,3},{5,0},{6,1},{7,2},{8,7},{9,4... | collective-permute-start | bytes 73736 | tf_op jit(solution)/shard_map/ppermute | solution.py:607
